TPU v7x, 32 devices: a whole 2x2x4 slice. The times are simulated.
32 devices in a mesh: members: 2 (over y), lat: 4 (over x, core), blk: 4 (over z).
Axes of the slice: x: 2, y: 2, z: 4, core: 2. Of those that a mesh axis runs over, the one named last changes fastest.
Arguments:
- starting_states: float32 [512, 256, 768], P(('members', 'blk'), 'lat'), may hold values from -6 to 6
- courant_x: float32 [256, 768], P('lat'), may hold values from -0.3 to 0.3
- courant_y: float32 [256, 768], P('lat'), may hold values from -0.3 to 0.3
- diffusion: float32 [256, 768], P('lat'), may hold values from 0.05 to 0.2
- obs_index: int32 [4, 8, 128], P('lat', ('members', 'blk')), may hold values from 0 to 6143
- obs_value: float32 [4, 8, 128], P('lat', ('members', 'blk')), may hold values from -6 to 6
- loc_weight: float32 [4, 8, 3, 128], P('lat', ('members', 'blk')), may hold values from 0.1 to 1
Outputs:
- analysis: float32 [512, 256, 768], P(('members', 'blk'), 'lat')
Inputs may be any that keep to these rules, and one draw needn't show every extreme that they name: `obs_index`: positions among the 6144 cells of the block, counted row by row; repeats may occur.
All inputs are finite; a program needn't handle non-finite values.
Results may differ from a plain program's by a relative error of at most 0.0003.
Values sent between devices are 32-bit elements; how exact they have to be, the bound alone decides.
No kernel may reach another device: no remote copies, remote signals or barrier semaphores. Data moves between devices by JAX's collectives and lax.ppermute only.
A program may use at most 128 MiB of HBM per device.

v0:
```python
import jax
import jax.numpy as jnp
from jax import lax
from jax.sharding import PartitionSpec as P

FSTEPS = 8
NS_ITERS = 4


HIGH = lax.Precision.HIGHEST


def extended(block, sides, width):
    for axis, dim in sides:
        count = lax.axis_size(axis)
        forward = [(i, i + 1) for i in range(count - 1)]
        backward = [(target, source) for source, target in forward]
        low = lax.ppermute(
            lax.slice_in_dim(block, block.shape[dim] - width, None, axis=dim), axis, forward
        )
        high = lax.ppermute(lax.slice_in_dim(block, 0, width, axis=dim), axis, backward)
        block = jnp.concatenate([low, block, high], axis=dim)
    return block


def passed_along(array, axis, by):
    size = lax.axis_size(axis)
    pairs = [(i, i + by) for i in range(size) if 0 <= i + by < size]
    return lax.ppermute(array, axis, pairs)


def advance(padded, coeffs):
    centre = padded[:, 1:-1]
    row_above = padded[:, 2:]
    row_below = padded[:, :-2]
    eastward_column = jnp.roll(centre, -1, axis=2)
    col_west = jnp.roll(centre, 1, axis=2)
    return (
        centre
        + 0.5 * coeffs[0] * (col_west - eastward_column)
        + 0.5 * coeffs[1] * (row_below - row_above)
        + coeffs[2] * (eastward_column + col_west + row_above + row_below - 4.0 * centre)
    )


def transform(block, stacked_members, innovation, weights):
    realization_number = block.shape[0]
    centre = jnp.mean(block, axis=0)
    anomaly = block - centre
    weighted = stacked_members * weights
    identity = jnp.eye(realization_number, dtype=jnp.float32)
    gram = identity + jnp.dot(weighted, stacked_members.T, precision=HIGH) / (
        realization_number - 1
    )
    frobenius = jnp.sqrt(jnp.sum(gram * gram) + 1e-06)
    iterate = gram / frobenius
    inverse = identity
    for repeat in range(NS_ITERS):
        factor = 1.5 * identity - 0.5 * jnp.dot(inverse, iterate, precision=HIGH)
        iterate = jnp.dot(iterate, factor, precision=HIGH)
        inverse = jnp.dot(factor, inverse, precision=HIGH)
    inv_root = inverse / jnp.sqrt(frobenius)
    pull_term = jnp.dot(weighted, innovation, precision=HIGH)
    shift_mean = jnp.dot(inv_root, jnp.dot(inv_root, pull_term, precision=HIGH), precision=HIGH) / (
        realization_number - 1
    )
    mixing = inv_root + shift_mean[:, None]
    return centre[None, :] + jnp.dot(mixing.T, anomaly, precision=HIGH)


def on_device(starting_states, courant_x, courant_y, diffusion, obs_index, obs_value, loc_weight):
    set_size, row_count, lon_count = starting_states.shape
    coeffs = jnp.stack([courant_x, courant_y, diffusion])
    field_now = starting_states
    for repeat in range(FSTEPS):
        padded = extended(field_now, (("lat", 1),), 1)
        field_now = advance(padded, coeffs)
    block = lax.all_to_all(field_now, ("members", "blk"), split_axis=1, concat_axis=0, tiled=True)
    realization_number, block_rows, lon_count = block.shape
    cells_flat = block.reshape(realization_number, block_rows * lon_count)
    positions = obs_index.reshape(-1)
    ybank = jnp.take(cells_flat, positions, axis=1)
    ybar = jnp.mean(ybank, axis=0)
    anom_own = ybank - ybar
    innov_own = obs_value.reshape(-1) - ybar
    received = []
    for offset in (1, -1):
        received.append(passed_along((anom_own, innov_own), ("members", "blk"), offset))
    stacked_members = jnp.concatenate([received[0][0], anom_own, received[1][0]], axis=1)
    innovation = jnp.concatenate([received[0][1], innov_own, received[1][1]], axis=0)
    weights = loc_weight.reshape(-1)
    corrected_states = transform(cells_flat, stacked_members, innovation, weights).reshape(
        realization_number, block_rows, lon_count
    )
    return lax.all_to_all(
        corrected_states, ("members", "blk"), split_axis=0, concat_axis=1, tiled=True
    )


def solution(mesh):
    in_specs = (
        P(("members", "blk"), "lat", None),
        P("lat", None),
        P("lat", None),
        P("lat", None),
        P("lat", ("members", "blk"), None),
        P("lat", ("members", "blk"), None),
        P("lat", ("members", "blk"), None, None),
    )
    out_specs = P(("members", "blk"), "lat", None)
    return jax.shard_map(
        on_device, mesh=mesh, in_specs=in_specs, out_specs=out_specs, check_vma=False
    )
```

profile of v0, /device:TPU:0, one launch (start us, length us, event | category | flops | bytes accessed | tf_op | source)
XLA Modules:
  0.0 1118.6 jit_solution(7278472649663360195)
XLA Ops:
  0.0 16.6 %copy.15 = f32[64,64,768]{2,0,1:T(8,128)} copy(f32[64,64,768]{2,1,0:T(8,128)} %param.7) | data formatting | bytes 25165824 | tf_op args[0]
  17.7 2.4 collective-permute-start
  20.1 1.6 collective-permute-start.1
  21.8 20.9 %fusion.44 = (f32[64,64,767]{2,0,1:T(8,128)}, f32[64,64,767]{2,0,1:T(8,128)}) fusion(f32[64,64,768]{2,0,1:T(8,128)} %copy.15), kind=kLoop, calls=%fused_computation.111 | loop fusion | bytes 50266112 | tf_op jit(solution)/shard_map/jit(_roll_static)/slice | solution.py:37
  42.7 5.1 fusion.43
  48.6 23.4 %multiply_add_fusion.7 = f32[64,64,768]{2,0,1:T(8,128)S(1)} fusion(f32[64,64,768]{2,0,1:T(8,128)} %copy.15, f32[64,1,768]{2,0,1:T(8,128)} %copy-done.4, f32[64,1,768]{2,0,1:T(8,128)} %copy-done.5, f32[64,64,1]{2,0,1:T(8,128)} %get-tuple-element.48, f32[64,64,767]{2,0,1:T(8,128)} %get-tuple-element.50, f32[64,64,767]{2,0,1:T(8,128)} %get-tuple-element.49, ...), kind=kLoop, calls=%fused_computation.44 | loop fusion | flops 53477376 | bytes 51314688 | tf_op jit(solution)/shard_map/add | solution.py:39
  72.0 10.2 fusion.41
  82.2 5.8 collective-permute-start.2
  88.0 1.7 collective-permute-start.3
  89.7 2.8 fusion.40
  92.6 18.9 %multiply_add_fusion.6 = f32[64,64,768]{2,0,1:T(8,128)} fusion(f32[64,64,768]{2,0,1:T(8,128)S(1)} %multiply_add_fusion.7, f32[64,1,768]{2,0,1:T(8,128)} %collective-permute-done.2, f32[64,1,768]{2,0,1:T(8,128)} %collective-permute-done.3, f32[64,64,1]{2,0,1:T(8,128)} %get-tuple-element.42, f32[64,64,767]{2,0,1:T(8,128)} %get-tuple-element.44, ...), kind=kLoop, calls=%fused_computation.43 | loop fusion | flops 53477376 | bytes 51314688 | tf_op jit(solution)/shard_map/add | solution.py:39
  111.4 22.2 %fusion.38 = (f32[64,64,767]{2,0,1:T(8,128)}, f32[64,64,767]{2,0,1:T(8,128)}) fusion(f32[64,64,768]{2,0,1:T(8,128)} %multiply_add_fusion.6), kind=kLoop, calls=%fused_computation.105 | loop fusion | bytes 50266112 | tf_op jit(solution)/shard_map/jit(_roll_static)/slice | solution.py:37
  133.6 6.2 collective-permute-start.4
  141.1 2.8 fusion.37
  143.9 18.9 %multiply_add_fusion.5 = f32[64,64,768]{2,0,1:T(8,128)} fusion(f32[64,64,768]{2,0,1:T(8,128)S(1)} %copy-done, f32[64,1,768]{2,0,1:T(8,128)} %collective-permute-done.4, f32[64,1,768]{2,0,1:T(8,128)} %collective-permute-done.5, f32[64,64,1]{2,0,1:T(8,128)} %get-tuple-element.36, f32[64,64,767]{2,0,1:T(8,128)} %get-tuple-element.38, ...), kind=kLoop, calls=%fused_computation.42 | loop fusion | flops 53477376 | bytes 51314688 | tf_op jit(solution)/shard_map/add | solution.py:39
  162.8 22.2 %fusion.35 = (f32[64,64,767]{2,0,1:T(8,128)}, f32[64,64,767]{2,0,1:T(8,128)}) fusion(f32[64,64,768]{2,0,1:T(8,128)} %multiply_add_fusion.5), kind=kLoop, calls=%fused_computation.102 | loop fusion | bytes 50266112 | tf_op jit(solution)/shard_map/jit(_roll_static)/slice | solution.py:37
  185.0 4.9 collective-permute-start.6
  189.8 1.5 collective-permute-start.7
  191.3 2.8 fusion.34
  194.2 18.9 %multiply_add_fusion.4 = f32[64,64,768]{2,0,1:T(8,128)} fusion(f32[64,64,768]{2,0,1:T(8,128)S(1)} %copy-done.1, f32[64,1,768]{2,0,1:T(8,128)} %collective-permute-done.6, f32[64,1,768]{2,0,1:T(8,128)} %collective-permute-done.7, f32[64,64,1]{2,0,1:T(8,128)} %get-tuple-element.30, f32[64,64,767]{2,0,1:T(8,128)} %get-tuple-element.32, ...), kind=kLoop, calls=%fused_computation.41 | loop fusion | flops 53477376 | bytes 51314688 | tf_op jit(solution)/shard_map/add | solution.py:39
  213.0 22.2 %fusion.32 = (f32[64,64,767]{2,0,1:T(8,128)}, f32[64,64,767]{2,0,1:T(8,128)}) fusion(f32[64,64,768]{2,0,1:T(8,128)} %multiply_add_fusion.4), kind=kLoop, calls=%fused_computation.99 | loop fusion | bytes 50266112 | tf_op jit(solution)/shard_map/jit(_roll_static)/slice | solution.py:37
  235.2 4.7 collective-permute-start.8
  241.2 2.8 fusion.31
  244.0 18.9 %multiply_add_fusion.3 = f32[64,64,768]{2,0,1:T(8,128)} fusion(f32[64,64,768]{2,0,1:T(8,128)S(1)} %copy-done.2, f32[64,1,768]{2,0,1:T(8,128)} %collective-permute-done.8, f32[64,1,768]{2,0,1:T(8,128)} %collective-permute-done.9, f32[64,64,1]{2,0,1:T(8,128)} %get-tuple-element.24, f32[64,64,767]{2,0,1:T(8,128)} %get-tuple-element.26, ...), kind=kLoop, calls=%fused_computation.40 | loop fusion | flops 53477376 | bytes 51314688 | tf_op jit(solution)/shard_map/add | solution.py:39
  262.9 22.2 %fusion.29 = (f32[64,64,767]{2,0,1:T(8,128)}, f32[64,64,767]{2,0,1:T(8,128)}) fusion(f32[64,64,768]{2,0,1:T(8,128)} %multiply_add_fusion.3), kind=kLoop, calls=%fused_computation.96 | loop fusion | bytes 50266112 | tf_op jit(solution)/shard_map/jit(_roll_static)/slice | solution.py:37
  285.1 4.9 collective-permute-start.10
  289.9 1.7 collective-permute-start.11
  291.6 2.8 fusion.28
  294.5 18.9 %multiply_add_fusion.2 = f32[64,64,768]{2,0,1:T(8,128)} fusion(f32[64,64,768]{2,0,1:T(8,128)S(1)} %copy-done.3, f32[64,1,768]{2,0,1:T(8,128)} %collective-permute-done.10, f32[64,1,768]{2,0,1:T(8,128)} %collective-permute-done.11, f32[64,64,1]{2,0,1:T(8,128)} %get-tuple-element.18, f32[64,64,767]{2,0,1:T(8,128)} %get-tuple-element.20, ...), kind=kLoop, calls=%fused_computation.39 | loop fusion | flops 53477376 | bytes 51314688 | tf_op jit(solution)/shard_map/add | solution.py:39
  313.3 21.0 %fusion.26 = (f32[64,64,767]{2,0,1:T(8,128)}, f32[64,64,767]{2,0,1:T(8,128)}) fusion(f32[64,64,768]{2,0,1:T(8,128)} %multiply_add_fusion.2), kind=kLoop, calls=%fused_computation.93 | loop fusion | bytes 50266112 | tf_op jit(solution)/shard_map/jit(_roll_static)/slice | solution.py:37
  335.4 3.8 collective-permute-start.12
  339.1 1.3 collective-permute-start.13
  340.4 5.2 fusion.25
  346.4 23.4 %multiply_add_fusion.1 = f32[64,64,768]{2,0,1:T(8,128)S(1)} fusion(f32[64,64,768]{2,0,1:T(8,128)} %multiply_add_fusion.2, f32[64,1,768]{2,0,1:T(8,128)} %copy-done.6, f32[64,1,768]{2,0,1:T(8,128)} %copy-done.7, f32[64,64,1]{2,0,1:T(8,128)} %get-tuple-element.12, f32[64,64,767]{2,0,1:T(8,128)} %get-tuple-element.14, f32[64,64,767]{2,0,1:T(8,128)} %get-tuple-element.13, ...), kind=kLoop, calls=%fused_computation.38 | loop fusion | flops 53477376 | bytes 51314688 | tf_op jit(solution)/shard_map/add | solution.py:39
  369.8 10.2 fusion.23
  379.9 3.7 collective-permute-start.14
  385.0 2.8 fusion.22
  387.8 18.9 %multiply_add_fusion = f32[64,64,768]{2,0,1:T(8,128)} fusion(f32[64,64,768]{2,0,1:T(8,128)S(1)} %multiply_add_fusion.1, f32[64,1,768]{2,0,1:T(8,128)} %collective-permute-done.14, f32[64,1,768]{2,0,1:T(8,128)} %collective-permute-done.15, f32[64,64,1]{2,0,1:T(8,128)} %get-tuple-element.6, f32[64,64,767]{2,0,1:T(8,128)} %get-tuple-element.8, ...), kind=kLoop, calls=%fused_computation.37 | loop fusion | flops 53477376 | bytes 51314688 | tf_op jit(solution)/shard_map/add | solution.py:39
  406.7 6.1 all-to-all-start
  412.9 272.8 %all-to-all-done = f32[64,64,768]{2,0,1:T(8,128)} async-done(((f32[64,64,768]{2,0,1:T(8,128)}), f32[64,64,768]{2,0,1:T(8,128)}, u32[]{:S(2)}, u32[]{:S(2)}) %all-to-all-start) | async-done | bytes 12582944 | tf_op jit(solution)/shard_map/all_to_all | solution.py:78
  685.7 16.4 %copy.21 = f32[64,8,8,768]{3,2,0,1:T(8,128)} copy(f32[64,8,8,768]{3,0,2,1:T(8,128)} %bitcast) | data formatting | bytes 25165824 | tf_op jit(solution)/shard_map/all_to_all | solution.py:78
  702.2 15.4 %copy.24 = f32[64,8,8,768]{3,1,2,0:T(8,128)} copy(f32[64,8,8,768]{3,2,1,0:T(8,128)} %bitcast.59) | data formatting | bytes 25165824
  717.5 12.6 %copy.22 = f32[512,6144]{0,1:T(8,128)} copy(f32[512,6144]{1,0:T(8,128)} %bitcast.55) | data formatting | bytes 25165824 | tf_op jit(solution)/shard_map/reshape | solution.py:80
  730.1 5.4 gather_fusion
  735.8 1.3 collective-permute-start.18
  737.1 1.3 collective-permute-start.19
  738.5 5.0 collective-permute-start.16
  743.6 1.3 collective-permute-start.17
  744.9 11.1 bitcast_reduce_fusion
  756.0 4.2 collective-permute-done.17
  760.2 2.6 multiply_reduce_fusion
  764.7 1.9 fusion.16
  767.8 1.9 select_subtract_fusion.2
  769.6 1.8 fusion.47
  771.5 1.8 fusion.46
  773.3 1.8 select_subtract_fusion.1
  775.2 1.8 fusion.49
  777.0 1.8 fusion.48
  778.9 1.8 select_subtract_fusion
  780.8 1.8 convolution_divide_fusion
  785.3 25.2 %fusion.2 = f32[512,6144]{1,0:T(8,128)} fusion(f32[512,6144]{1,0:T(8,128)} %bitcast.56, f32[6144]{0:T(1024)S(1)} %div.40, f32[512,512]{1,0:T(8,128)S(1)} %convolution_divide_fusion, f32[512]{0:T(512)S(1)} %broadcast_multiply_fusion.3), kind=kOutput, calls=%fused_computation.45 | convolution fusion | flops 19333906432 | bytes 26241024 | tf_op jit(solution)/shard_map/dot_general | solution.py:68
  810.4 15.0 %copy.25 = f32[64,8,8,768]{3,2,1,0:T(8,128)} copy(f32[64,8,8,768]{3,1,2,0:T(8,128)} %bitcast.60) | data formatting | bytes 25165824
  825.4 281.6 %all_to_all.33 = f32[512,8,768]{2,1,0:T(8,128)} all-to-all(f32[512,8,768]{2,1,0:T(8,128)} %bitcast.57), channel_id=1, replica_groups=mesh['members'=2,'lat'=4,'blk'=4] {'members','blk'}, dimensions={0} | all-to-all | bytes 25165824 | tf_op jit(solution)/shard_map/all_to_all | solution.py:95
  1107.0 11.2 %copy.28 = f32[8,64,8,768]{3,2,0,1:T(8,128)} copy(f32[8,64,8,768]{3,2,1,0:T(8,128)} %bitcast.58) | data formatting | bytes 25165824 | tf_op jit(solution)/shard_map/all_to_all | solution.py:95
  (74 shorter events, 12.9 us)
Async XLA Ops:
  17.7 30.1 %collective-permute-start = (f32[64,1,768]{2,0,1:T(8,128)S(1)}, f32[64,1,768]{2,0,1:T(8,128)S(1)}, u32[]{:S(2)}, u32[]{:S(2)}) collective-permute-start(f32[64,1,768]{2,0,1:T(8,128)S(1)} %get-tuple-element.52), channel_id=1, source_target_pairs={{0,4},{4,8},{8,12},{1,5},{5,9},{9,13},{2,6},{6,10},{10,14},{3,7},{... | collective-permute-start | bytes 589832 | tf_op jit(solution)/shard_map/ppermute | solution.py:18
  20.1 27.7 %copy-start.8 = (f32[64,768]{1,0:T(8,128)S(1)}, f32[64,768]{1,0:T(8,128)}, u32[]{:S(2)}) copy-start(f32[64,768]{1,0:T(8,128)} %param.9) | copy-start | bytes 589828
  20.1 27.6 %copy-start.9 = (f32[64,768]{1,0:T(8,128)S(1)}, f32[64,768]{1,0:T(8,128)}, u32[]{:S(2)}) copy-start(f32[64,768]{1,0:T(8,128)} %param.8) | copy-start | bytes 589828
  20.1 27.7 %collective-permute-start.1 = (f32[64,1,768]{2,0,1:T(8,128)S(1)}, f32[64,1,768]{2,0,1:T(8,128)S(1)}, u32[]{:S(2)}, u32[]{:S(2)}) collective-permute-start(f32[64,1,768]{2,0,1:T(8,128)S(1)} %get-tuple-element.51), channel_id=1, source_target_pairs={{4,0},{8,4},{12,8},{5,1},{9,5},{13,9},{6,2},{10,6},{14,10},{7,3},{... | collective-permute-start | bytes 589832 | tf_op jit(solution)/shard_map/ppermute | solution.py:21
  47.8 0.7 copy-start.4
  47.8 0.7 copy-start.5
  82.2 10.4 collective-permute-start.2
  88.0 4.5 collective-permute-start.3
  111.4 22.2 %copy-start = (f32[64,64,768]{2,0,1:T(8,128)S(1)}, f32[64,64,768]{2,0,1:T(8,128)}, u32[]{:S(2)}) copy-start(f32[64,64,768]{2,0,1:T(8,128)} %multiply_add_fusion.6) | copy-start | bytes 37748740
  133.6 10.3 collective-permute-start.4
  139.8 4.1 collective-permute-start.5
  162.8 22.2 %copy-start.1 = (f32[64,64,768]{2,0,1:T(8,128)S(1)}, f32[64,64,768]{2,0,1:T(8,128)}, u32[]{:S(2)}) copy-start(f32[64,64,768]{2,0,1:T(8,128)} %multiply_add_fusion.5) | copy-start | bytes 37748740
  185.0 9.2 collective-permute-start.6
  189.8 4.3 collective-permute-start.7
  213.0 22.2 %copy-start.2 = (f32[64,64,768]{2,0,1:T(8,128)S(1)}, f32[64,64,768]{2,0,1:T(8,128)}, u32[]{:S(2)}) copy-start(f32[64,64,768]{2,0,1:T(8,128)} %multiply_add_fusion.4) | copy-start | bytes 37748740
  235.2 8.8 collective-permute-start.8
  239.9 4.1 collective-permute-start.9
  262.9 22.2 %copy-start.3 = (f32[64,64,768]{2,0,1:T(8,128)S(1)}, f32[64,64,768]{2,0,1:T(8,128)}, u32[]{:S(2)}) copy-start(f32[64,64,768]{2,0,1:T(8,128)} %multiply_add_fusion.3) | copy-start | bytes 37748740
  285.1 9.4 collective-permute-start.10
  289.9 4.5 collective-permute-start.11
  335.4 10.2 collective-permute-start.12
  339.1 6.5 collective-permute-start.13
  345.6 0.7 copy-start.6
  345.6 0.8 copy-start.7
  379.9 7.9 collective-permute-start.14
  383.7 4.1 collective-permute-start.15
  406.7 6.1 copy-start.10
  406.7 6.2 copy-start.12
  406.7 279.1 %all-to-all-start = ((f32[64,64,768]{2,0,1:T(8,128)}), f32[64,64,768]{2,0,1:T(8,128)}, u32[]{:S(2)}, u32[]{:S(2)}) async-start(f32[64,64,768]{2,0,1:T(8,128)} %multiply_add_fusion), calls=%async_computation | async-start | bytes 25165824 | tf_op jit(solution)/shard_map/all_to_all | solution.py:78
  717.5 18.2 %copy-start.11 = (f32[1,1,128]{2,1,0:T(1,128)S(1)}, f32[1,1,128]{2,1,0:T(1,128)}, u32[]{:S(2)}) copy-start(f32[1,1,128]{2,1,0:T(1,128)} %param.12) | copy-start | bytes 1540
  735.8 20.2 %collective-permute-start.18 = (f32[128]{0:T(128)S(1)}, f32[128]{0:T(128)S(1)}, u32[]{:S(2)}, u32[]{:S(2)}) collective-permute-start(f32[128]{0:T(128)S(1)} %get-tuple-element.53), channel_id=1, source_target_pairs={{0,1},{1,2},{2,3},{3,16},{16,17},{17,18},{18,19},{4,5},{5,6},{6,7}... | collective-permute-start | bytes 1544 | tf_op jit(solution)/shard_map/ppermute | solution.py:29
  737.1 18.9 %collective-permute-start.19 = (f32[128]{0:T(128)S(1)}, f32[128]{0:T(128)S(1)}, u32[]{:S(2)}, u32[]{:S(2)}) collective-permute-start(f32[128]{0:T(128)S(1)} %get-tuple-element.53), channel_id=1, source_target_pairs={{1,0},{2,1},{3,2},{16,3},{17,16},{18,17},{19,18},{5,4},{6,5},{7,6}... | collective-permute-start | bytes 1544 | tf_op jit(solution)/shard_map/ppermute | solution.py:29
  738.5 17.5 %collective-permute-start.16 = (f32[512,128]{0,1:T(8,128)S(1)}, f32[512,128]{0,1:T(8,128)S(1)}, u32[]{:S(2)}, u32[]{:S(2)}) collective-permute-start(f32[512,128]{0,1:T(8,128)S(1)} %subtract_bitcast_fusion), channel_id=1, source_target_pairs={{0,1},{1,2},{2,3},{3,16},{16,17},{17,18},{18,19},{4,5},{5,6},{6,7}... | collective-permute-start | bytes 786440 | tf_op jit(solution)/shard_map/ppermute | solution.py:29
  743.6 16.7 %collective-permute-start.17 = (f32[512,128]{0,1:T(8,128)S(1)}, f32[512,128]{0,1:T(8,128)S(1)}, u32[]{:S(2)}, u32[]{:S(2)}) collective-permute-start(f32[512,128]{0,1:T(8,128)S(1)} %subtract_bitcast_fusion), channel_id=1, source_target_pairs={{1,0},{2,1},{3,2},{16,3},{17,16},{18,17},{19,18},{5,4},{6,5},{7,6}... | collective-permute-start | bytes 786440 | tf_op jit(solution)/shard_map/ppermute | solution.py:29
where the time goes:
time: 1130 us; the launch traced here: 1120 us
  blocking collectives  282 us (25%)
  waiting for transfers between devices  277 us (25%)
  local copies, waits for them, and re-layouts  275 us (24%)
  other arithmetic  171 us (15%)
  starting transfers between devices  63 us (6%)
  matrix products  49.4 us (4%)
    all_to_all x1, blocking collectives, on_device(): lax.all_to_all(corrected_states, ('members', 'blk'), split_axis=0, concat...  282 us
    all_to_all x1, waiting for transfers between devices, on_device(): lax.all_to_all(field_now, ('members', 'blk'), split_axis=1, concat_axis=0...  273 us
    slice x16, local copies, waits for them, and re-layouts, advance(): col_west = jnp.roll(centre, 1, axis=2)  178 us
    add x8, other arithmetic, advance(): centre + 0.5 * coeffs[0] * (col_west - eastward_column)  160 us
    unnamed x29, local copies, waits for them, and re-layouts  48.5 us
    ppermute x8, starting transfers between devices, extended(): lax.ppermute(lax.slice_in_dim(block, block.shape[dim] - width, None, axis...  36.3 us
    dot_general x1, matrix products, transform(): return centre[None, :] + jnp.dot(mixing.T, anomaly, precision=HIGH)  25.2 us
  transfers between devices with their start and end apart: 21, of which 2 were waited for; matrix products, arithmetic and copies ran while one was open for 5% of the time, Pallas kernels for 0%

commit v1 on v0

v1 whole, which is shorter than its diff:
```python
import functools
import jax
import jax.numpy as jnp
from jax import lax
from jax.experimental import pallas as pl
from jax.experimental.pallas import tpu as pltpu
from jax.sharding import PartitionSpec as P


FSTEPS = 8
NS_ITERS = 4
LANES = 128

HIGH = lax.Precision.HIGHEST
GROUP = ("members", "blk")
F32 = jnp.float32
BF16 = jnp.bfloat16


def call(kernel, flops, moved, **kwargs):
    return pl.pallas_call(
        kernel,
        compiler_params=pltpu.CompilerParams(vmem_limit_bytes=48 << 20),
        cost_estimate=pl.CostEstimate(flops=flops, bytes_accessed=moved, transcendentals=0),
        **kwargs,
    )


def shifted(array, axis, by):
    size = lax.axis_size(axis)
    pairs = [(i, i + by) for i in range(size) if 0 <= i + by < size]
    return lax.ppermute(array, axis, pairs)


def forecast_body(unroll, x_ref, low_ref, high_ref, coeff_ref, y_ref, even_ref, odd_ref):
    rows, _, lon = y_ref.shape
    halo = FSTEPS
    total = rows + 2 * halo
    even_ref[0:halo] = jnp.swapaxes(low_ref[...], 0, 1)
    even_ref[halo + rows :] = jnp.swapaxes(high_ref[...], 0, 1)
    for first in range(0, rows, 8):
        even_ref[halo + first : halo + first + 8] = jnp.swapaxes(
            x_ref[:, first : first + 8, :], 0, 1
        )
    src, dst = even_ref, odd_ref
    for step in range(FSTEPS):
        first, last = step + 1, total - 1 - step

        def advance(row, src=src, dst=dst, final=step == FSTEPS - 1):
            here = src[row]
            east = pltpu.roll(here, lon - 1, 1)
            west = pltpu.roll(here, 1, 1)
            c = [coeff_ref[k, pl.ds(row, 1), :] for k in range(5)]
            new = c[0] * here + c[1] * west + c[2] * east + c[3] * src[row - 1] + c[4] * src[row + 1]
            if final:
                y_ref[row - halo] = new
            else:
                dst[row] = new

        def several(i, carry, first=first, advance=advance):
            for k in range(unroll):
                advance(first + i * unroll + k)
            return carry

        trips = (last - first) // unroll
        lax.fori_loop(0, trips, several, 0)
        for row in range(first + trips * unroll, last):
            advance(row)
        src, dst = dst, src


def forecast(x, low, high, coeffs, start, halo_start, count):
    _, rows, lon = x.shape
    group = 16 if count % 16 == 0 and start % 16 == 0 and halo_start % 16 == 0 else 8
    total = coeffs.shape[1]
    return call(
        functools.partial(forecast_body, 8),
        flops=9 * FSTEPS * total * count * lon,
        moved=8 * count * rows * lon,
        grid=(count // group,),
        in_specs=[
            pl.BlockSpec((group, rows, lon), lambda i: (start // group + i, 0, 0)),
            pl.BlockSpec((group, FSTEPS, lon), lambda i: (halo_start // group + i, 0, 0)),
            pl.BlockSpec((group, FSTEPS, lon), lambda i: (halo_start // group + i, 0, 0)),
            pl.BlockSpec((5, total, lon), lambda i: (0, 0, 0)),
        ],
        out_specs=pl.BlockSpec((rows, group, lon), lambda i: (0, i, 0)),
        out_shape=jax.ShapeDtypeStruct((rows, count, lon), F32),
        scratch_shapes=[pltpu.VMEM((total, group, lon), F32)] * 2,
    )(x, low, high, coeffs)


def split3(value):
    top = value.astype(BF16)
    rest = value - top.astype(F32)
    middle = rest.astype(BF16)
    return top, middle, (rest - middle.astype(F32)).astype(BF16)


def observe_body(cells_ref, *refs):
    chunks, out_ref = refs[:-1], refs[-1]
    block_rows, _, lon = chunks[0].shape
    obs = cells_ref.shape[-1]
    count = out_ref.shape[1]
    total = jnp.zeros((3 * count, obs), F32)
    place = lax.broadcasted_iota(jnp.int32, (lon, obs), 0)
    for row in range(block_rows):
        field = jnp.concatenate([ref[row] for ref in chunks], axis=0)
        chosen = jnp.where(place + row * lon == cells_ref[0], 1.0, 0.0).astype(BF16)
        total += jnp.dot(
            jnp.concatenate(split3(field), axis=0), chosen, preferred_element_type=F32
        )
    out_ref[0] = total[:count] + total[count : 2 * count] + total[2 * count :]


def observe(chunks, cells):
    rows, _, lon = chunks[0].shape
    blocks, _, obs = cells.shape
    block_rows = rows // blocks
    count = sum(chunk.shape[1] for chunk in chunks)
    return call(
        observe_body,
        flops=6 * count * rows * lon * obs,
        moved=4 * count * rows * lon,
        grid=(blocks,),
        in_specs=[pl.BlockSpec((1, 1, obs), lambda k: (k, 0, 0))]
        + [
            pl.BlockSpec((block_rows, chunk.shape[1], lon), lambda k: (k, 0, 0)) for chunk in chunks
        ],
        out_specs=pl.BlockSpec((1, count, obs), lambda k: (k, 0, 0)),
        out_shape=jax.ShapeDtypeStruct((blocks, count, obs), F32),
    )(cells, *chunks)


def mixing_body(layout, banks_ref, values_ref, weights_ref, mix_high_ref, mix_low_ref):
    sources, _, wide = banks_ref.shape
    size = mix_high_ref.shape[0]
    pieces = []
    for start, count in layout:
        for source in range(sources):
            pieces.append(banks_ref[source, start : start + count, :])
    bank = jnp.concatenate(pieces, axis=0)
    mean = jnp.sum(bank, axis=0, keepdims=True) / size
    stacked = bank - mean
    innovation = values_ref[...] - mean
    weighted = stacked * weights_ref[...]

    def dot(a, b, contract=((1,), (0,))):
        return lax.dot_general(a, b, (contract, ((), ())), precision=HIGH, preferred_element_type=F32)

    shape = (size, size)
    identity = jnp.where(
        lax.broadcasted_iota(jnp.int32, shape, 0) == lax.broadcasted_iota(jnp.int32, shape, 1), 1.0, 0.0
    )
    gram = identity + dot(weighted, stacked, ((1,), (1,))) / (size - 1)
    squares = jnp.sum(jnp.sum(gram * gram, axis=0, keepdims=True), axis=1, keepdims=True)
    frobenius = jnp.sqrt(squares + 1e-06)
    iterate = gram / frobenius
    inverse = 1.5 * identity - 0.5 * iterate
    iterate = dot(iterate, inverse)
    for repeat in range(1, NS_ITERS):
        factor = 1.5 * identity - 0.5 * dot(inverse, iterate)
        if repeat < NS_ITERS - 1:
            iterate = dot(iterate, factor)
        inverse = dot(factor, inverse)
    inv_root = inverse / jnp.sqrt(frobenius)
    wide_row = jnp.broadcast_to(innovation, (8, wide))
    pull = dot(wide_row, weighted, ((1,), (1,)))
    shift = (dot(dot(pull, inv_root), inv_root) / (size - 1))[:1]
    mixing = inv_root + shift
    mixing = mixing + (1.0 - jnp.sum(mixing, axis=1, keepdims=True)) / size
    top = mixing.astype(BF16)
    mix_high_ref[...] = top
    mix_low_ref[...] = (mixing - top.astype(F32)).astype(BF16)


def mixing_matrix(banks, values, weights, layout):
    sources, count, wide = banks.shape
    size = sources * count
    out = jax.ShapeDtypeStruct((size, size), BF16)
    return call(
        functools.partial(mixing_body, layout),
        flops=6 * 2 * 10 * size * size * size,
        moved=4 * size * (wide + size),
        out_shape=(out, out),
    )(banks, values, weights)


def analyse_body(layout, mix_high_ref, mix_low_ref, *refs):
    chunks, out_ref = refs[:-1], refs[-1]
    lanes = out_ref.shape[-1]
    field = jnp.concatenate(
        [ref[:, 0].reshape(ref.shape[0] * ref.shape[2], lanes) for ref in chunks], axis=0
    )
    top = field.astype(BF16)
    low = (field - top.astype(F32)).astype(BF16)

    def dot(a, b):
        return jnp.dot(a, b, preferred_element_type=F32)

    mix_high = mix_high_ref[...]
    result = dot(mix_high, top) + (dot(mix_high, low) + dot(mix_low_ref[...], top))
    at = 0
    targets = out_ref.shape[0]
    for start, count in layout:
        for target in range(targets):
            out_ref[target, 0, start : start + count, :] = result[at : at + count]
            at += count


def analyse(mix_high, mix_low, chunks, layout, first, lanes):
    sources, block_rows, _, _ = chunks[0].shape
    count = sum(chunk.shape[2] for chunk in chunks)
    size = sources * count
    return call(
        functools.partial(analyse_body, layout),
        flops=6 * size * size * block_rows * lanes,
        moved=8 * size * block_rows * lanes,
        grid=(block_rows,),
        in_specs=[pl.BlockSpec((size, size), lambda r: (0, 0))] * 2
        + [
            pl.BlockSpec((sources, 1, chunk.shape[2], lanes), lambda r: (0, r, 0, first // lanes))
            for chunk in chunks
        ],
        out_specs=pl.BlockSpec((sources, 1, count, lanes), lambda r: (0, r, 0, 0)),
        out_shape=jax.ShapeDtypeStruct((sources, block_rows, count, lanes), F32),
    )(mix_high, mix_low, *chunks)


def place_body(part_ref, *refs):
    out_ref = refs[-1]
    rows = out_ref.shape[1]
    for first in range(0, rows, 8):
        out_ref[:, first : first + 8, :] = jnp.swapaxes(part_ref[first : first + 8], 0, 1)


def place(part, whole, first, lon):
    rows, count, lanes = part.shape
    group = 16 if count % 16 == 0 else 8
    out = jax.ShapeDtypeStruct((count, rows, lon), F32)
    return call(
        place_body,
        flops=0,
        moved=8 * rows * count * lanes,
        grid=(count // group,),
        in_specs=[pl.BlockSpec((rows, group, lanes), lambda i: (0, i, 0))]
        + ([] if whole is None else [pl.BlockSpec(memory_space=pl.ANY)]),
        out_specs=pl.BlockSpec((group, rows, lanes), lambda i: (i, 0, first // lanes)),
        out_shape=out,
        input_output_aliases={} if whole is None else {1: 0},
    )(*((part,) if whole is None else (part, whole)))


def member_chunks(count):
    if count == 64:
        return (8, 8, 16, 32)
    return (count,)


def lane_chunks(lon):
    tiles = lon // LANES
    if tiles == 6:
        return (256, 256, 128, 128)
    return (lon,)


def exchange(array):
    return lax.all_to_all(array, GROUP, split_axis=0, concat_axis=0, tiled=True)


def on_device(starting_states, courant_x, courant_y, diffusion, obs_index, obs_value, loc_weight):
    members, rows, lon = starting_states.shape
    blocks = lax.axis_size("members") * lax.axis_size("blk")
    block_rows = rows // blocks
    obs = obs_index.shape[-1]
    counts = member_chunks(members)
    starts = [sum(counts[:i]) for i in range(len(counts))]
    layout = tuple(zip(starts, counts))
    halo = FSTEPS

    def edges(states):
        return shifted(states[:, rows - halo :], "lat", 1), shifted(states[:, :halo], "lat", -1)

    fields = jnp.stack([courant_x, courant_y, diffusion])
    head = sum(counts[:2])
    ends = jnp.concatenate([starting_states[:head, rows - halo :], fields[:, rows - halo :]])
    low = shifted(ends, "lat", 1)
    ends = jnp.concatenate([starting_states[:head, :halo], fields[:, :halo]])
    high = shifted(ends, "lat", -1)
    fields = jnp.concatenate([low[head:], fields, high[head:]], axis=1)
    across, along, spread = 0.5 * fields[0], 0.5 * fields[1], fields[2]
    coeffs = jnp.stack(
        [1.0 - 4.0 * spread, across + spread, spread - across, along + spread, spread - along]
    )

    states, received = [], []
    halos = low[:head], high[:head]
    for i, (start, count) in enumerate(layout):
        early = start < head
        state = forecast(
            starting_states, *halos, coeffs, start, start - (0 if early else head), count
        )
        states.append(state)
        if i == 0 and head < members:
            later, state = lax.optimization_barrier((starting_states, state))
            halos_rest = edges(later[head:])
        if i == 1:
            halos = halos_rest
    local = jnp.concatenate([obs_index.reshape(1, obs).astype(F32), obs_value.reshape(1, obs)])
    local, _ = lax.optimization_barrier((local, states[-1]))
    everyone = lax.all_gather(local[None], GROUP, axis=0, tiled=True)
    for state in states[:-1]:
        received.append(exchange(state.reshape(blocks, block_rows, -1, lon)))

    cells = everyone[:, :1].astype(jnp.int32)
    own = observe(states, cells)
    zero = jnp.zeros((1,) + own.shape[1:], F32)
    triple = jnp.concatenate(
        [jnp.concatenate([zero, own[:-1]]), own, jnp.concatenate([own[1:], zero])], axis=2
    )
    banks = exchange(triple)
    received.append(exchange(states[-1].reshape(blocks, block_rows, -1, lon)))

    zero = jnp.zeros((1, obs), F32)
    values = jnp.concatenate([zero, everyone[:, 1], zero])
    values = lax.dynamic_slice_in_dim(values, lax.axis_index(GROUP), 3).reshape(1, 3 * obs)
    mix_high, mix_low = mixing_matrix(banks, values, loc_weight.reshape(1, 3 * obs), layout)

    result, first = None, 0
    for lanes in lane_chunks(lon):
        part = analyse(mix_high, mix_low, received, layout, first, lanes)
        part = exchange(part)
        result = place(part.reshape(rows, members, lanes), result, first, lon)
        first += lanes
    return result


def solution(mesh):
    in_specs = (
        P(GROUP, "lat", None),
        P("lat", None),
        P("lat", None),
        P("lat", None),
        P("lat", GROUP, None),
        P("lat", GROUP, None),
        P("lat", GROUP, None, None),
    )

    return jax.shard_map(
        on_device, mesh=mesh, in_specs=in_specs, out_specs=P(GROUP, "lat", None), check_vma=False
    )
```

time: 1130 us -> 801 us (0.71)
  local copies, waits for them, and re-layouts: 275 us -> 14.4 us
  Pallas kernels: 0 us -> 181 us
  other arithmetic: 171 us -> 0.35 us
  blocking collectives: 282 us -> 209 us
  waiting for transfers between devices: 277 us -> 349 us
  matrix products: 49.4 us -> 0 us
  starting transfers between devices: 63 us -> 36.8 us
    pallas_call x0 -> x14, Pallas kernels: none -> 181 us  [the longest x4 103 us: forecast(): call(functools.partial(forecast_body, 8), flops=9 * FSTEPS * total * coun...]
    slice x24 -> x7, local copies, waits for them, and re-layouts: 180 us -> 3.12 us  [the longest x1 1.79 us: edges(): states[:, :halo]]
    add x8 -> x0, other arithmetic: 160 us -> none  [advance(): centre + 0.5 * coeffs[0] * (col_west - eastward_column)]
    all_to_all x1 -> x4, blocking collectives: 282 us -> 176 us  [exchange(): return lax.all_to_all(array, GROUP, split_axis=0, concat_axis=0, tiled=True)]
    all_to_all x1 -> x5, waiting for transfers between devices: 273 us -> 348 us  [exchange(): return lax.all_to_all(array, GROUP, split_axis=0, concat_axis=0, tiled=True)]
    dot_general x16 -> x0, matrix products: 49.4 us -> none  [the longest x1 25.2 us: transform(): return centre[None, :] + jnp.dot(mixing.T, anomaly, precision=HIGH)]
    ppermute x20 -> x4, starting transfers between devices: 56.8 us -> 14.9 us  [shifted(): return lax.ppermute(array, axis, pairs)]
    unnamed x29 -> x37, local copies, waits for them, and re-layouts: 48.5 us -> 11.2 us
  transfers between devices with their start and end apart: 21 -> 9, of which waited for: 2 -> 6; matrix products, arithmetic and copies ran while one was open for 5% -> 0% of each run, Pallas kernels for 0% -> 9%
where the time goes in v1:
time: 801 us; the launch traced here: 792 us
  waiting for transfers between devices  349 us (44%)
  blocking collectives  209 us (26%)
  Pallas kernels  181 us (23%)
  starting transfers between devices  36.8 us (5%)
  local copies, waits for them, and re-layouts  14.4 us (2%)
    all_to_all x5, waiting for transfers between devices, exchange(): return lax.all_to_all(array, GROUP, split_axis=0, concat_axis=0, tiled=True)  348 us
    all_to_all x4, blocking collectives, exchange(): return lax.all_to_all(array, GROUP, split_axis=0, concat_axis=0, tiled=True)  176 us
    pallas_call x4, Pallas kernels, forecast(): call(functools.partial(forecast_body, 8), flops=9 * FSTEPS * total * coun...  103 us
    all_gather x1, blocking collectives, on_device(): everyone = lax.all_gather(local[None], GROUP, axis=0, tiled=True)  33.1 us
    pallas_call x4, Pallas kernels, analyse(): call(functools.partial(analyse_body, layout), flops=6 * size * size * blo...  32.7 us
    all_to_all x5, starting transfers between devices, exchange(): return lax.all_to_all(array, GROUP, split_axis=0, concat_axis=0, tiled=True)  21.9 us
    pallas_call x1, Pallas kernels, mixing_matrix(): call(functools.partial(mixing_body, layout), flops=6 * 2 * 10 * size * si...  19.9 us
  transfers between devices with their start and end apart: 9, of which 6 were waited for; matrix products, arithmetic and copies ran while one was open for 0% of the time, Pallas kernels for 9%

profile of v1, /device:TPU:0, one launch (start us, length us, event | category | flops | bytes accessed | tf_op | source)
XLA Modules:
  0.0 791.7 jit_solution(17657312685156622018)
XLA Ops:
  0.0 1.2 fusion.6
  1.2 0.0 copy-done.13
  1.2 0.0 copy-done.14
  1.3 0.1 copy-done.15
  1.4 0.1 fusion
  1.4 1.3 collective-permute-start.1
  2.7 3.1 collective-permute-start
  5.8 0.0 collective-permute-done.1
  5.8 1.4 collective-permute-done
  7.2 0.1 pad_maximum_fusion
  7.5 15.1 %shard_map.73.refs_0_ = f32[64,8,768]{2,1,0:T(8,128)S(1)} custom-call(f32[64,64,768]{2,1,0:T(8,128)} %x_ref.7, f32[16,8,768]{2,1,0:T(8,128)S(1)} %slice.71.low_ref, f32[16,8,768]{2,1,0:T(8,128)S(1)} %slice.72.high_ref, f32[5,80,768]{2,1,0:T(8,128)S(1)} %subtract_dynamic-update-slice_fusion.coeff_ref), custom_call_target="tpu_custom_call" | custom-call | flops 35389440 | bytes 3145728 | tf_op jit(solution)/shard_map/pallas_call | solution.py:76
  22.6 0.0 copy-start.17
  22.6 0.0 copy-start.16
  22.6 1.8 fusion.5
  24.4 1.3 collective-permute-start.3
  25.7 9.2 %collective-permute-start.2 = (f32[48,8,768]{2,1,0:T(8,128)S(1)}, f32[48,8,768]{2,1,0:T(8,128)S(1)}, u32[]{:S(2)}, u32[]{:S(2)}) collective-permute-start(f32[48,8,768]{2,1,0:T(8,128)S(1)} %get-tuple-element.14), channel_id=1, source_target_pairs={{0,4},{4,8},{8,12},{1,5},{5,9},{9,13},{2,6},{6,10},{10,14},{3,7},{... | collective-permute-start | bytes 3538952 | tf_op jit(solution)/shard_map/ppermute | solution.py:32
  35.0 0.0 copy-done.17
  35.0 0.0 copy-done.16
  35.0 15.1 %shard_map.75.refs_1_ = f32[64,8,768]{2,1,0:T(8,128)S(1)} custom-call(f32[64,64,768]{2,1,0:T(8,128)} %x_ref.7, f32[16,8,768]{2,1,0:T(8,128)S(1)} %slice.71.low_ref, f32[16,8,768]{2,1,0:T(8,128)S(1)} %slice.72.high_ref, f32[5,80,768]{2,1,0:T(8,128)S(1)} %subtract_dynamic-update-slice_fusion.coeff_ref), custom_call_target="tpu_custom_call" | custom-call | flops 35389440 | bytes 3145728 | tf_op jit(solution)/shard_map/pallas_call | solution.py:76
  50.1 0.0 collective-permute-done.3.high_ref
  50.1 0.0 collective-permute-done.2.low_ref
  50.1 47.4 %shard_map.74.refs_3_ = f32[64,32,768]{2,1,0:T(8,128)} custom-call(f32[64,64,768]{2,1,0:T(8,128)} %x_ref.7, f32[48,8,768]{2,1,0:T(8,128)S(1)} %collective-permute-done.2.low_ref, f32[48,8,768]{2,1,0:T(8,128)S(1)} %collective-permute-done.3.high_ref, f32[5,80,768]{2,1,0:T(8,128)S(1)} %subtract_dynamic-update-slice_fusion.coeff_ref), custom_call_target="tpu_custom_call" | custom-call | flops 141557760 | bytes 12582912 | tf_op jit(solution)/shard_map/pallas_call | solution.py:76
  97.5 33.1 %all-gather.1 = f32[8,2,128]{2,1,0:T(2,128)S(1)} all-gather(f32[1,2,128]{2,1,0:T(2,128)S(1)} %bitcast.37), channel_id=2, replica_groups=mesh['members'=2,'lat'=4,'blk'=4] {'members','blk'}, dimensions={0}, use_global_device_ids=true | all-gather | bytes 9216 | tf_op jit(solution)/shard_map/all_gather | solution.py:311
  130.6 25.4 %shard_map.76.refs_2_ = f32[64,16,768]{2,1,0:T(8,128)} custom-call(f32[64,64,768]{2,1,0:T(8,128)} %x_ref.7, f32[48,8,768]{2,1,0:T(8,128)S(1)} %collective-permute-done.2.low_ref, f32[48,8,768]{2,1,0:T(8,128)S(1)} %collective-permute-done.3.high_ref, f32[5,80,768]{2,1,0:T(8,128)S(1)} %subtract_dynamic-update-slice_fusion.coeff_ref), custom_call_target="tpu_custom_call" | custom-call | flops 70778880 | bytes 6291456 | tf_op jit(solution)/shard_map/pallas_call | solution.py:76
  156.1 9.6 %shard_map.77 = f32[8,64,128]{2,1,0:T(8,128)S(1)} custom-call(s32[8,1,128]{2,1,0:T(1,128)S(1)} %get-tuple-element.22.cells_ref, f32[64,8,768]{2,1,0:T(8,128)S(1)} %shard_map.73.refs_0_, f32[64,8,768]{2,1,0:T(8,128)S(1)} %shard_map.75.refs_1_, f32[64,16,768]{2,1,0:T(8,128)} %shard_map.76.refs_2_, f32[64,32,768]{2,1,0:T(8,128)} %shard_map.74.refs_3_), custom_call_target="tpu_custom_call" | custom-call | flops 2415919104 | bytes 12582912 | tf_op jit(solution)/shard_map/pallas_call | solution.py:121
  165.8 0.1 select_maximum_fusion
  165.8 23.2 %all_to_all.45.banks_ref = f32[8,64,384]{2,1,0:T(8,128)} all-to-all(f32[8,64,384]{2,1,0:T(8,128)S(1)} %select_maximum_fusion), channel_id=1, replica_groups=mesh['members'=2,'lat'=4,'blk'=4] {'members','blk'}, dimensions={0} | all-to-all | bytes 1572864 | tf_op jit(solution)/shard_map/all_to_all | solution.py:268
  189.1 39.2 %all_to_all.46.refs_0_ = f32[8,8,8,768]{3,2,1,0:T(8,128)S(1)} all-to-all(f32[8,8,8,768]{3,2,1,0:T(8,128)S(1)} %bitcast.23), channel_id=1, replica_groups=mesh['members'=2,'lat'=4,'blk'=4] {'members','blk'}, dimensions={0} | all-to-all | bytes 3145728 | tf_op jit(solution)/shard_map/all_to_all | solution.py:268
  228.2 39.4 %all_to_all.47.refs_1_ = f32[8,8,8,768]{3,2,1,0:T(8,128)S(1)} all-to-all(f32[8,8,8,768]{3,2,1,0:T(8,128)S(1)} %bitcast.24), channel_id=1, replica_groups=mesh['members'=2,'lat'=4,'blk'=4] {'members','blk'}, dimensions={0} | all-to-all | bytes 3145728 | tf_op jit(solution)/shard_map/all_to_all | solution.py:268
  267.7 0.0 copy-done.12
  267.7 73.8 %all_to_all.48.refs_2_ = f32[8,8,16,768]{3,2,1,0:T(8,128)} all-to-all(f32[8,8,16,768]{3,2,1,0:T(8,128)S(1)} %bitcast.29), channel_id=1, replica_groups=mesh['members'=2,'lat'=4,'blk'=4] {'members','blk'}, dimensions={0} | all-to-all | bytes 6291456 | tf_op jit(solution)/shard_map/all_to_all | solution.py:268
  341.5 4.9 all-to-all-start.4
  346.4 0.0 copy-done.11
  346.4 0.0 copy-start.10
  346.4 1.1 copy-done.10
  347.6 19.9 %shard_map.78 = (bf16[512,512]{1,0:T(8,128)(2,1)S(1)}, bf16[512,512]{1,0:T(8,128)(2,1)S(1)}) custom-call(f32[8,64,384]{2,1,0:T(8,128)S(1)} %copy-done.10, f32[1,384]{1,0:T(1,128)S(1)} %bitcast.26, f32[1,384]{1,0:T(1,128)S(1)} %bitcast.27), custom_call_target="tpu_custom_call" | custom-call | flops 16106127360 | bytes 1835008 | tf_op jit(solution)/shard_map/pallas_call | solution.py:181
  367.4 0.0 copy-start
  367.5 0.8 copy-done
  368.3 0.8 copy-done.5
  369.1 115.1 %all-to-all-done.4.refs_3_ = f32[8,8,32,768]{3,2,1,0:T(8,128)} async-done(((f32[8,8,32,768]{3,2,1,0:T(8,128)}), f32[8,8,32,768]{3,2,1,0:T(8,128)}, u32[]{:S(2)}, u32[]{:S(2)}) %all-to-all-start.4) | async-done | bytes 6291488 | tf_op jit(solution)/shard_map/all_to_all | solution.py:268
  484.2 1.0 copy-done.1
  485.2 1.0 copy-done.6
  486.3 7.8 shard_map.80
  494.1 4.3 all-to-all-start.6
  498.4 1.0 copy-done.2
  499.5 1.0 copy-done.7
  500.5 8.6 %shard_map.81 = f32[8,8,64,256]{3,2,1,0:T(8,128)} custom-call(bf16[512,512]{1,0:T(8,128)(2,1)S(1)} %copy-done.2, bf16[512,512]{1,0:T(8,128)(2,1)S(1)} %copy-done.7, f32[8,8,8,768]{3,2,1,0:T(8,128)S(1)} %all_to_all.46.refs_0_, f32[8,8,8,768]{3,2,1,0:T(8,128)S(1)} %all_to_all.47.refs_1_, f32[8,8,16,768]{3,2,1,0:T(8,128)} %all_to_all.48.refs_2_, ...), custom_call_target="tpu_custom_call" | custom-call | flops 3221225472 | bytes 8388608 | tf_op jit(solution)/shard_map/pallas_call | solution.py:215
  509.1 36.5 %all-to-all-done.6 = f32[8,8,64,128]{3,2,1,0:T(8,128)} async-done(((f32[8,8,64,128]{3,2,1,0:T(8,128)}), f32[8,8,64,128]{3,2,1,0:T(8,128)}, u32[]{:S(2)}, u32[]{:S(2)}) %all-to-all-start.6) | async-done | bytes 2097184 | tf_op jit(solution)/shard_map/all_to_all | solution.py:268
  545.5 4.6 all-to-all-start.7
  550.1 1.0 copy-done.3
  551.1 1.0 copy-done.8
  552.2 8.5 %shard_map.82 = f32[8,8,64,256]{3,2,1,0:T(8,128)} custom-call(bf16[512,512]{1,0:T(8,128)(2,1)S(1)} %copy-done.3, bf16[512,512]{1,0:T(8,128)(2,1)S(1)} %copy-done.8, f32[8,8,8,768]{3,2,1,0:T(8,128)S(1)} %all_to_all.46.refs_0_, f32[8,8,8,768]{3,2,1,0:T(8,128)S(1)} %all_to_all.47.refs_1_, f32[8,8,16,768]{3,2,1,0:T(8,128)} %all_to_all.48.refs_2_, ...), custom_call_target="tpu_custom_call" | custom-call | flops 3221225472 | bytes 8388608 | tf_op jit(solution)/shard_map/pallas_call | solution.py:215
  560.7 81.0 %all-to-all-done.7 = f32[8,8,64,256]{3,2,1,0:T(8,128)} async-done(((f32[8,8,64,256]{3,2,1,0:T(8,128)}), f32[8,8,64,256]{3,2,1,0:T(8,128)}, u32[]{:S(2)}, u32[]{:S(2)}) %all-to-all-start.7) | async-done | bytes 4194336 | tf_op jit(solution)/shard_map/all_to_all | solution.py:268
  641.8 4.5 all-to-all-start.8
  646.3 1.0 copy-done.4
  647.4 1.0 copy-done.9
  648.4 7.8 shard_map.79
  656.2 81.8 %all-to-all-done.8 = f32[8,8,64,256]{3,2,1,0:T(8,128)} async-done(((f32[8,8,64,256]{3,2,1,0:T(8,128)}), f32[8,8,64,256]{3,2,1,0:T(8,128)}, u32[]{:S(2)}, u32[]{:S(2)}) %all-to-all-start.8) | async-done | bytes 4194336 | tf_op jit(solution)/shard_map/all_to_all | solution.py:268
  738.0 3.6 all-to-all-start.5
  741.6 5.0 shard_map.83.refs_0_
  746.6 5.0 shard_map.84.refs_0_
  751.6 3.9 shard_map.85.refs_0_
  755.5 33.7 %all-to-all-done.5 = f32[8,8,64,128]{3,2,1,0:T(8,128)S(1)} async-done(((f32[8,8,64,128]{3,2,1,0:T(8,128)}), f32[8,8,64,128]{3,2,1,0:T(8,128)S(1)}, u32[]{:S(2)}, u32[]{:S(2)}) %all-to-all-start.5) | async-done | bytes 2097184 | tf_op jit(solution)/shard_map/all_to_all | solution.py:268
  789.2 2.1 shard_map.86
  (30 shorter events, 0.3 us)
Async XLA Ops:
  0.0 1.2 copy-start.13
  0.0 1.3 copy-start.14
  0.0 1.3 copy-start.15
  1.4 4.4 collective-permute-start.1
  2.7 4.5 collective-permute-start
  22.6 12.4 %copy-start.17 = (s32[1,1,128]{2,1,0:T(1,128)S(1)}, s32[1,1,128]{2,1,0:T(1,128)}, u32[]{:S(2)}) copy-start(s32[1,1,128]{2,1,0:T(1,128)} %param.11) | copy-start | bytes 1540
  22.6 12.4 %copy-start.16 = (f32[1,1,128]{2,1,0:T(1,128)S(1)}, f32[1,1,128]{2,1,0:T(1,128)}, u32[]{:S(2)}) copy-start(f32[1,1,128]{2,1,0:T(1,128)} %param.12) | copy-start | bytes 1540
  24.4 25.7 %collective-permute-start.3 = (f32[48,8,768]{2,1,0:T(8,128)S(1)}, f32[48,8,768]{2,1,0:T(8,128)S(1)}, u32[]{:S(2)}, u32[]{:S(2)}) collective-permute-start(f32[48,8,768]{2,1,0:T(8,128)S(1)} %get-tuple-element.13), channel_id=1, source_target_pairs={{4,0},{8,4},{12,8},{5,1},{9,5},{13,9},{6,2},{10,6},{14,10},{7,3},{... | collective-permute-start | bytes 3538952 | tf_op jit(solution)/shard_map/ppermute | solution.py:32
  25.7 24.4 %collective-permute-start.2 = (f32[48,8,768]{2,1,0:T(8,128)S(1)}, f32[48,8,768]{2,1,0:T(8,128)S(1)}, u32[]{:S(2)}, u32[]{:S(2)}) collective-permute-start(f32[48,8,768]{2,1,0:T(8,128)S(1)} %get-tuple-element.14), channel_id=1, source_target_pairs={{0,4},{4,8},{8,12},{1,5},{5,9},{9,13},{2,6},{6,10},{10,14},{3,7},{... | collective-permute-start | bytes 3538952 | tf_op jit(solution)/shard_map/ppermute | solution.py:32
  228.2 39.4 %copy-start.12 = (f32[64,16,768]{2,1,0:T(8,128)S(1)}, f32[64,16,768]{2,1,0:T(8,128)}, u32[]{:S(2)}) copy-start(f32[64,16,768]{2,1,0:T(8,128)} %shard_map.76.refs_2_) | copy-start | bytes 9437188
  341.5 4.9 copy-start.11
  341.5 142.7 %all-to-all-start.4 = ((f32[8,8,32,768]{3,2,1,0:T(8,128)}), f32[8,8,32,768]{3,2,1,0:T(8,128)}, u32[]{:S(2)}, u32[]{:S(2)}) async-start(f32[8,8,32,768]{3,2,1,0:T(8,128)} %bitcast.28), calls=%async_computation.4 | async-start | bytes 12582912 | tf_op jit(solution)/shard_map/all_to_all | solution.py:268
  346.4 1.1 copy-start.10
  367.4 0.8 copy-start
  368.3 0.8 copy-start.5
  484.2 1.0 copy-start.1
  485.2 1.0 copy-start.6
  494.1 51.5 %all-to-all-start.6 = ((f32[8,8,64,128]{3,2,1,0:T(8,128)}), f32[8,8,64,128]{3,2,1,0:T(8,128)}, u32[]{:S(2)}, u32[]{:S(2)}) async-start(f32[8,8,64,128]{3,2,1,0:T(8,128)} %shard_map.80), calls=%async_computation.6 | async-start | bytes 4194304 | tf_op jit(solution)/shard_map/all_to_all | solution.py:268
  498.4 1.0 copy-start.2
  499.5 1.0 copy-start.7
  545.5 96.2 %all-to-all-start.7 = ((f32[8,8,64,256]{3,2,1,0:T(8,128)}), f32[8,8,64,256]{3,2,1,0:T(8,128)}, u32[]{:S(2)}, u32[]{:S(2)}) async-start(f32[8,8,64,256]{3,2,1,0:T(8,128)} %shard_map.81), calls=%async_computation.7 | async-start | bytes 8388608 | tf_op jit(solution)/shard_map/all_to_all | solution.py:268
  550.1 1.0 copy-start.3
  551.1 1.0 copy-start.8
  641.8 96.2 %all-to-all-start.8 = ((f32[8,8,64,256]{3,2,1,0:T(8,128)}), f32[8,8,64,256]{3,2,1,0:T(8,128)}, u32[]{:S(2)}, u32[]{:S(2)}) async-start(f32[8,8,64,256]{3,2,1,0:T(8,128)} %shard_map.82), calls=%async_computation.8 | async-start | bytes 8388608 | tf_op jit(solution)/shard_map/all_to_all | solution.py:268
  646.3 1.0 copy-start.4
  647.4 1.0 copy-start.9
  738.0 51.2 %all-to-all-start.5 = ((f32[8,8,64,128]{3,2,1,0:T(8,128)}), f32[8,8,64,128]{3,2,1,0:T(8,128)S(1)}, u32[]{:S(2)}, u32[]{:S(2)}) async-start(f32[8,8,64,128]{3,2,1,0:T(8,128)} %shard_map.79), calls=%async_computation.5 | async-start | bytes 4194304 | tf_op jit(solution)/shard_map/all_to_all | solution.py:268

commit v2 on v1

v2 whole, which is shorter than its diff:
```python
import functools
import jax
import jax.numpy as jnp
from jax import lax
from jax.experimental import pallas as pl
from jax.experimental.pallas import tpu as pltpu
from jax.sharding import PartitionSpec as P


FSTEPS = 8
NS_ITERS = 4
LANES = 128

HIGH = lax.Precision.HIGHEST
GROUP = ("members", "blk")
F32 = jnp.float32
BF16 = jnp.bfloat16


def call(kernel, flops, moved, **kwargs):
    return pl.pallas_call(
        kernel,
        compiler_params=pltpu.CompilerParams(vmem_limit_bytes=48 << 20),
        cost_estimate=pl.CostEstimate(flops=flops, bytes_accessed=moved, transcendentals=0),
        **kwargs,
    )


def shifted(array, axis, by):
    size = lax.axis_size(axis)
    pairs = [(i, i + by) for i in range(size) if 0 <= i + by < size]
    return lax.ppermute(array, axis, pairs)


UNROLL = 16


def forecast_body(x_ref, low_ref, high_ref, coeff_ref, *refs):
    outs, (even_ref, odd_ref) = refs[:-2], refs[-2:]
    _, rows, lon = x_ref.shape
    halo = FSTEPS
    even_ref[0:halo] = jnp.swapaxes(low_ref[...], 0, 1)
    even_ref[halo + rows : 2 * halo + rows] = jnp.swapaxes(high_ref[...], 0, 1)
    for first in range(0, rows, 8):
        even_ref[halo + first : halo + first + 8] = jnp.swapaxes(
            x_ref[:, first : first + 8, :], 0, 1
        )

    def advance(src, dst, first, count):
        def several(i, carry):
            for k in range(UNROLL):
                row = first + i * UNROLL + k
                here = src[row]
                east = pltpu.roll(here, lon - 1, 1)
                west = pltpu.roll(here, 1, 1)
                c = [coeff_ref[k, pl.ds(row, 1), :] for k in range(5)]
                dst[row] = (
                    c[0] * here + c[1] * west + c[2] * east + c[3] * src[row - 1] + c[4] * src[row + 1]
                )
            return carry

        lax.fori_loop(0, (count + UNROLL - 1) // UNROLL, several, 0)

    def two(k, carry):
        first = 2 * k + 1
        count = rows + 2 * halo - 2 * first
        advance(even_ref, odd_ref, first, count)
        advance(odd_ref, even_ref, first + 1, count - 2)
        return carry

    lax.fori_loop(0, FSTEPS // 2, two, 0)
    at = 0
    for out_ref in outs:
        lanes = out_ref.shape[-1]
        out_ref[...] = even_ref[halo : halo + rows, :, at : at + lanes]
        at += lanes


def forecast(x, low, high, coeffs, start, halo_start, count, widths):
    _, rows, lon = x.shape
    group = 16 if count % 16 == 0 and start % 16 == 0 and halo_start % 16 == 0 else 8
    total = coeffs.shape[1]
    return call(
        forecast_body,
        flops=9 * FSTEPS * total * count * lon,
        moved=8 * count * rows * lon,
        grid=(count // group,),
        in_specs=[
            pl.BlockSpec((group, rows, lon), lambda i: (start // group + i, 0, 0)),
            pl.BlockSpec((group, FSTEPS, lon), lambda i: (halo_start // group + i, 0, 0)),
            pl.BlockSpec((group, FSTEPS, lon), lambda i: (halo_start // group + i, 0, 0)),
            pl.BlockSpec((5, total, lon), lambda i: (0, 0, 0)),
        ],
        out_specs=[pl.BlockSpec((rows, group, lanes), lambda i: (0, i, 0)) for lanes in widths],
        out_shape=[pltpu.HBM((rows, count, lanes), F32) for lanes in widths],
        scratch_shapes=[pltpu.VMEM((total, group, lon), F32)] * 2,
    )(x, low, high, coeffs)


def split3(value):
    top = value.astype(BF16)
    rest = value - top.astype(F32)
    middle = rest.astype(BF16)
    return top, middle, (rest - middle.astype(F32)).astype(BF16)


def observe_body(parts, cells_ref, *refs):
    chunks, out_ref = list(refs[:-1]), refs[-1]
    block_rows = chunks[0].shape[0]
    chunks = [[chunks.pop(0) for _ in range(n)] for n in parts]
    lon = sum(ref.shape[-1] for ref in chunks[0])
    obs = cells_ref.shape[-1]
    count = out_ref.shape[1]
    total = jnp.zeros((3 * count, obs), F32)
    place = lax.broadcasted_iota(jnp.int32, (lon, obs), 0)
    for row in range(block_rows):
        field = jnp.concatenate(
            [jnp.concatenate([ref[row] for ref in refs], axis=1) for refs in chunks], axis=0
        )
        chosen = jnp.where(place + row * lon == cells_ref[0], 1.0, 0.0).astype(BF16)
        total += jnp.dot(
            jnp.concatenate(split3(field), axis=0), chosen, preferred_element_type=F32
        )
    out_ref[0] = total[:count] + total[count : 2 * count] + total[2 * count :]


def observe(chunks, cells):
    rows = chunks[0][0].shape[0]
    lon = sum(part.shape[-1] for part in chunks[0])
    blocks, _, obs = cells.shape
    block_rows = rows // blocks
    count = sum(chunk[0].shape[1] for chunk in chunks)
    flat = [part for chunk in chunks for part in chunk]
    return call(
        functools.partial(observe_body, tuple(len(chunk) for chunk in chunks)),
        flops=6 * count * rows * lon * obs,
        moved=4 * count * rows * lon,
        grid=(blocks,),
        in_specs=[pl.BlockSpec((1, 1, obs), lambda k: (k, 0, 0))]
        + [pl.BlockSpec((block_rows,) + part.shape[1:], lambda k: (k, 0, 0)) for part in flat],
        out_specs=pl.BlockSpec((1, count, obs), lambda k: (k, 0, 0)),
        out_shape=jax.ShapeDtypeStruct((blocks, count, obs), F32),
    )(cells, *flat)


def mixing_body(layout, banks_ref, values_ref, weights_ref, top_ref, low_ref, *scratch):
    stacked_ref, weighted_ref, one_ref, two_ref, factor_ref, inverse_ref = scratch
    sources = banks_ref.shape[0]
    size, wide = stacked_ref.shape
    at, start = 0, 0
    for _, count in layout:
        for source in range(sources):
            stacked_ref[at : at + count] = banks_ref[source, start : start + count, :]
            at += count
        start += count
    bank = stacked_ref[...]
    mean = jnp.sum(bank, axis=0, keepdims=True) / size
    stacked = bank - mean
    innovation = values_ref[...] - mean
    weighted = stacked * weights_ref[...]
    stacked_ref[...] = stacked
    weighted_ref[...] = weighted

    def dot(a, b, contract=((1,), (0,))):
        return lax.dot_general(a, b, (contract, ((), ())), precision=HIGH, preferred_element_type=F32)

    strip = size // 2

    def halves(value):
        top = value.astype(BF16)
        return top, (value - top.astype(F32)).astype(BF16)

    def product(dst, a, b, finish=None, contract=((1,), (0,))):
        def rows_of(i, carry):
            rows = pl.ds(pl.multiple_of(i * strip, strip), strip)
            (a_top, a_low), (b_top, b_low) = halves(a[rows, :]), halves(b[...])

            def part(x, y):
                return lax.dot_general(x, y, (contract, ((), ())), preferred_element_type=F32)

            value = part(a_top, b_top) + (part(a_top, b_low) + part(a_low, b_top))
            dst[rows, :] = value if finish is None else finish(i, value)
            return carry

        lax.fori_loop(0, size // strip, rows_of, 0)

    def unit(i, shape):
        row = lax.broadcasted_iota(jnp.int32, shape, 0) + i * strip
        return jnp.where(row == lax.broadcasted_iota(jnp.int32, shape, 1), 1.0, 0.0)

    product(
        one_ref,
        weighted_ref,
        stacked_ref,
        lambda i, value: unit(i, value.shape) + value / (size - 1),
        ((1,), (1,)),
    )
    gram = one_ref[...]
    squares = jnp.sum(jnp.sum(gram * gram, axis=0, keepdims=True), axis=1, keepdims=True)
    frobenius = jnp.sqrt(squares + 1e-06)
    iterate = gram / frobenius
    one_ref[...] = iterate
    inverse_ref[...] = 1.5 * unit(0, iterate.shape) - 0.5 * iterate
    product(two_ref, one_ref, inverse_ref)
    held, spare, inverse = two_ref, one_ref, inverse_ref
    for repeat in range(1, NS_ITERS):
        product(
            factor_ref, inverse, held, lambda i, value: 1.5 * unit(i, value.shape) - 0.5 * value
        )
        if repeat < NS_ITERS - 1:
            product(spare, held, factor_ref)
            held, spare = spare, held
        product(spare, factor_ref, inverse)
        inverse, spare = spare, inverse
    inv_root = inverse[...] / jnp.sqrt(frobenius)
    spare[...] = inv_root
    innovation = jnp.broadcast_to(innovation, (8, wide))
    pull = dot(innovation, weighted_ref[...], ((1,), (1,)))
    shift = (dot(dot(pull, inv_root), inv_root) / (size - 1))[:1]
    mixing = inv_root + shift
    mixing = mixing + (1.0 - jnp.sum(mixing, axis=1, keepdims=True)) / size
    top = mixing.astype(BF16)
    top_ref[...] = top
    low_ref[...] = (mixing - top.astype(F32)).astype(BF16)


def mixing_matrix(banks, values, weights, layout):
    sources, count, wide = banks.shape
    size = sources * count
    out = jax.ShapeDtypeStruct((size, size), BF16)
    return call(
        functools.partial(mixing_body, layout),
        flops=6 * 2 * 10 * size * size * size,
        moved=4 * size * (wide + size),
        out_shape=(out, out),
        scratch_shapes=[pltpu.VMEM((size, wide), F32)] * 2 + [pltpu.VMEM((size, size), F32)] * 4,
    )(banks, values, weights)


def analyse_body(layout, mix_top_ref, mix_low_ref, *refs):
    chunks, out_ref = refs[:-1], refs[-1]
    targets, rows, _, lanes = out_ref.shape
    field = jnp.concatenate(
        [
            jnp.concatenate(
                [ref[:, row].reshape(ref.shape[0] * ref.shape[2], lanes) for row in range(rows)], axis=1
            )
            for ref in chunks
        ],
        axis=0,
    )
    top = field.astype(BF16)
    low = (field - top.astype(F32)).astype(BF16)

    def dot(a, b):
        return jnp.dot(a, b, preferred_element_type=F32)

    mix_top = mix_top_ref[...]
    result = dot(mix_top, top) + (dot(mix_top, low) + dot(mix_low_ref[...], top))
    at = 0
    for start, count in layout:
        for target in range(targets):
            for row in range(rows):
                out_ref[target, row, start : start + count, :] = result[
                    at : at + count, row * lanes : (row + 1) * lanes
                ]
            at += count


def analyse(mix_top, mix_low, chunks, layout, lanes):
    sources, block_rows, _, _ = chunks[0][0].shape
    count = sum(chunk.shape[2] for chunk, _ in chunks)
    size = sources * count
    step = 2 if block_rows % 2 == 0 else 1

    def spec(chunk, first):
        return pl.BlockSpec(
            (sources, step, chunk.shape[2], lanes), lambda r: (0, r, 0, first // lanes)
        )

    return call(
        functools.partial(analyse_body, layout),
        flops=6 * size * size * block_rows * lanes,
        moved=8 * size * block_rows * lanes,
        grid=(block_rows // step,),
        in_specs=[pl.BlockSpec((size, size), lambda r: (0, 0))] * 2
        + [spec(chunk, first) for chunk, first in chunks],
        out_specs=pl.BlockSpec((sources, step, count, lanes), lambda r: (0, r, 0, 0)),
        out_shape=pltpu.HBM((sources, block_rows, count, lanes), F32),
    )(mix_top, mix_low, *[chunk for chunk, _ in chunks])


def place_body(part_ref, *refs):
    out_ref = refs[-1]
    rows = out_ref.shape[1]
    for first in range(0, rows, 8):
        out_ref[:, first : first + 8, :] = jnp.swapaxes(part_ref[first : first + 8], 0, 1)


def place(part, whole, first, lon):
    rows, count, lanes = part.shape
    group = 16 if count % 16 == 0 else 8
    out = jax.ShapeDtypeStruct((count, rows, lon), F32)
    return call(
        place_body,
        flops=0,
        moved=8 * rows * count * lanes,
        grid=(count // group,),
        in_specs=[pl.BlockSpec((rows, group, lanes), lambda i: (0, i, 0))]
        + ([] if whole is None else [pl.BlockSpec(memory_space=pl.ANY)]),
        out_specs=pl.BlockSpec((group, rows, lanes), lambda i: (i, 0, first // lanes)),
        out_shape=out,
        input_output_aliases={} if whole is None else {1: 0},
    )(*((part,) if whole is None else (part, whole)))


def member_chunks(count):
    if count > 24 and count % 16 == 0:
        return (count - 8, 8), (0, 16), (16, count - 24)
    return ((0, count),)


def lane_parts(lon):
    third = lon // 3
    return (2 * third, third) if lon % (3 * LANES) == 0 else (lon,)


def gathered(row):
    size, me = lax.axis_size("members") * lax.axis_size("blk"), lax.axis_index(GROUP)
    bit = 1
    while bit < size:
        other = lax.ppermute(row, GROUP, [(i, i ^ bit) for i in range(size)])
        row = jnp.where(
            (me & bit) == 0, jnp.concatenate([row, other]), jnp.concatenate([other, row])
        )
        bit *= 2
    return row


def exchange(array):
    return lax.all_to_all(array, GROUP, split_axis=0, concat_axis=0, tiled=True)


def exchange_by_steps(array):
    size, me = array.shape[0], lax.axis_index(GROUP)
    if size > 8 or size & (size - 1):
        return exchange(array)
    pieces = [lax.dynamic_slice_in_dim(array, me, 1)]
    for step in range(1, size):
        piece = lax.dynamic_slice_in_dim(array, me ^ step, 1)
        pieces.append(lax.ppermute(piece, GROUP, [(i, i ^ step) for i in range(size)]))
    pieces = jnp.concatenate(pieces)
    return jnp.concatenate([lax.dynamic_slice_in_dim(pieces, me ^ i, 1) for i in range(size)])


def on_device(starting_states, courant_x, courant_y, diffusion, obs_index, obs_value, loc_weight):
    members, rows, lon = starting_states.shape
    blocks = lax.axis_size("members") * lax.axis_size("blk")
    block_rows = rows // blocks
    obs = obs_index.shape[-1]
    layout = member_chunks(members)
    widths = lane_parts(lon)
    halo = FSTEPS

    def edges(states):
        return shifted(states[:, rows - halo :], "lat", 1), shifted(states[:, :halo], "lat", -1)

    fields = jnp.stack([courant_x, courant_y, diffusion])
    early = layout[:2]
    head = sum(count for _, count in early)

    def ends(first):
        return jnp.concatenate(
            [starting_states[at : at + count, first : first + halo] for at, count in early]
            + [fields[:, first : first + halo]]
        )

    low = shifted(ends(rows - halo), "lat", 1)
    high = shifted(ends(0), "lat", -1)
    local = jnp.concatenate([obs_index.reshape(1, obs).astype(F32), obs_value.reshape(1, obs)])
    everyone = gathered(local[None])
    spare = jnp.zeros((3, UNROLL + 8, lon), F32)
    fields = jnp.concatenate([low[head:], fields, high[head:], spare], axis=1)
    across, along, spread = 0.5 * fields[0], 0.5 * fields[1], fields[2]
    coeffs = jnp.stack(
        [1.0 - 4.0 * spread, across + spread, spread - across, along + spread, spread - along]
    )

    states = []
    halos, at = (low[:head], high[:head]), 0
    for i, (start, count) in enumerate(layout):
        parts = widths if i == len(layout) - 1 else (lon,)
        if i == 2:
            halos, at = halos_rest, 0
        state = forecast(starting_states, *halos, coeffs, start, at, count, parts)
        at += count
        states.append(state)
        if i == 0 and len(layout) > 2:
            later, _ = lax.optimization_barrier((starting_states, state[0]))
            halos_rest = edges(later[layout[2][0] : layout[2][0] + layout[2][1]])
    received = []
    for i, state in enumerate(states):
        received.append([])
        for part in state:
            received[i].append(exchange(part.reshape(blocks, block_rows, *part.shape[1:])))

    cells = everyone[:, :1].astype(jnp.int32)
    own = observe(states, cells)
    zero = jnp.zeros((1,) + own.shape[1:], F32)
    triple = jnp.concatenate(
        [jnp.concatenate([zero, own[:-1]]), own, jnp.concatenate([own[1:], zero])], axis=2
    )
    banks = exchange_by_steps(triple)
    zero = jnp.zeros((1, obs), F32)
    values = jnp.concatenate([zero, everyone[:, 1], zero])
    values = lax.dynamic_slice_in_dim(values, lax.axis_index(GROUP), 3).reshape(1, 3 * obs)
    mix_top, mix_low = mixing_matrix(banks, values, loc_weight.reshape(1, 3 * obs), layout)

    result, first = None, 0
    for j, lanes in enumerate(widths):
        chunks = [(chunk[0], first) if len(chunk) == 1 else (chunk[j], 0) for chunk in received]
        part = analyse(mix_top, mix_low, chunks, layout, lanes)
        part = exchange(part)
        result = place(part.reshape(rows, members, lanes), result, first, lon)
        first += lanes
    return result


def solution(mesh):
    in_specs = (
        P(GROUP, "lat", None),
        P("lat", None),
        P("lat", None),
        P("lat", None),
        P("lat", GROUP, None),
        P("lat", GROUP, None),
        P("lat", GROUP, None, None),
    )

    return jax.shard_map(
        on_device, mesh=mesh, in_specs=in_specs, out_specs=P(GROUP, "lat", None), check_vma=False
    )
```

time: 801 us -> 673 us (0.84)
  blocking collectives: 209 us -> 0 us
  waiting for transfers between devices: 349 us -> 424 us
  starting transfers between devices: 36.8 us -> 75.3 us
  Pallas kernels: 181 us -> 163 us
    all_to_all x4 -> x0, blocking collectives: 176 us -> none  [exchange(): return lax.all_to_all(array, GROUP, split_axis=0, concat_axis=0, tiled=True)]
    ppermute x0 -> x10, waiting for transfers between devices: none -> 156 us  [the longest x3 103 us: gathered(): other = lax.ppermute(row, GROUP, [(i, i ^ bit) for i in range(size)])]
    all_to_all x5 -> x6, waiting for transfers between devices: 348 us -> 264 us  [exchange(): return lax.all_to_all(array, GROUP, split_axis=0, concat_axis=0, tiled=True)]
    all_gather x1 -> x0, blocking collectives: 33.1 us -> none  [on_device(): everyone = lax.all_gather(local[None], GROUP, axis=0, tiled=True)]
    ppermute x0 -> x10, starting transfers between devices: none -> 22 us  [the longest x7 13.6 us: exchange_by_steps(): lax.ppermute(piece, GROUP, [(i, i ^ step) for i in range(size)])]
    all_to_all x5 -> x6, starting transfers between devices: 21.9 us -> 42.2 us  [exchange(): return lax.all_to_all(array, GROUP, split_axis=0, concat_axis=0, tiled=True)]
    pallas_call x4 -> x2, Pallas kernels: 32.7 us -> 17.4 us  [analyse(): call(functools.partial(analyse_body, layout), flops=6 * size * size * blo...]
    pallas_call x5 -> x4, Pallas kernels: 113 us -> 118 us  [the longest x3 109 us: forecast(): call(forecast_body, flops=9 * FSTEPS * total * count * lon, moved=8 * cou...]
  transfers between devices with their start and end apart: 9 -> 20, of which waited for: 6 -> 12; matrix products, arithmetic and copies ran while one was open for 0% -> 0% of each run, Pallas kernels for 9% -> 21%
where the time goes in v2:
time: 673 us; the launch traced here: 671 us
  waiting for transfers between devices  424 us (63%)
  Pallas kernels  163 us (24%)
  starting transfers between devices  75.3 us (11%)
  local copies, waits for them, and re-layouts  8.31 us (1%)
    all_to_all x6, waiting for transfers between devices, exchange(): return lax.all_to_all(array, GROUP, split_axis=0, concat_axis=0, tiled=True)  264 us
    pallas_call x3, Pallas kernels, forecast(): call(forecast_body, flops=9 * FSTEPS * total * count * lon, moved=8 * cou...  109 us
    ppermute x3, waiting for transfers between devices, gathered(): other = lax.ppermute(row, GROUP, [(i, i ^ bit) for i in range(size)])  103 us
    ppermute x7, waiting for transfers between devices, exchange_by_steps(): lax.ppermute(piece, GROUP, [(i, i ^ step) for i in range(size)])  53.2 us
    all_to_all x6, starting transfers between devices, exchange(): return lax.all_to_all(array, GROUP, split_axis=0, concat_axis=0, tiled=True)  42.2 us
    pallas_call x2, Pallas kernels, analyse(): call(functools.partial(analyse_body, layout), flops=6 * size * size * blo...  17.4 us
    pallas_call x1, Pallas kernels, mixing_matrix(): call(functools.partial(mixing_body, layout), flops=6 * 2 * 10 * size * si...  14.7 us
    ppermute x7, starting transfers between devices, exchange_by_steps(): lax.ppermute(piece, GROUP, [(i, i ^ step) for i in range(size)])  13.6 us
  transfers between devices with their start and end apart: 20, of which 12 were waited for; matrix products, arithmetic and copies ran while one was open for 0% of the time, Pallas kernels for 21%

profile of v2, /device:TPU:0, one launch (start us, length us, event | category | flops | bytes accessed | tf_op | source)
XLA Modules:
  0.0 671.3 jit_solution(12400397852092139738)
XLA Ops:
  0.0 1.1 fusion.6
  1.1 1.2 fusion.7
  2.3 0.1 fusion
  2.4 1.3 collective-permute-start.4
  3.7 3.1 collective-permute-start.3
  6.8 0.1 pad.13.clone
  6.9 0.0 collective-permute-done.4
  6.9 1.6 collective-permute-done.3
  8.5 0.1 maximum_maximum_fusion
  8.9 0.0 copy-start.4
  9.0 15.5 %shard_map.73.refs_0_ = f32[64,8,768]{2,1,0:T(8,128)} custom-call(f32[64,64,768]{2,1,0:T(8,128)} %x_ref.5, f32[24,8,768]{2,1,0:T(8,128)S(1)} %slice.80.low_ref, f32[24,8,768]{2,1,0:T(8,128)S(1)} %slice.81.high_ref, f32[5,104,768]{2,1,0:T(8,128)S(1)} %subtract_dynamic-update-slice_fusion.coeff_ref), custom_call_target="tpu_custom_call" | custom-call | flops 46006272 | bytes 3145728 | tf_op jit(solution)/shard_map/pallas_call | solution.py:83
  24.5 0.0 copy-done.2
  24.5 7.3 %all-to-all-start = ((f32[8,8,8,768]{3,2,1,0:T(8,128)}), f32[8,8,8,768]{3,2,1,0:T(8,128)S(1)}, u32[]{:S(2)}, u32[]{:S(2)}) async-start(f32[8,8,8,768]{3,2,1,0:T(8,128)} %bitcast.22), calls=%async_computation | async-start | bytes 3145728 | tf_op jit(solution)/shard_map/all_to_all | solution.py:341
  31.8 1.1 copy-done.3
  32.9 1.1 copy-done.5
  34.0 27.8 %shard_map.74.refs_1_ = f32[64,16,768]{2,1,0:T(8,128)} custom-call(f32[64,64,768]{2,1,0:T(8,128)} %x_ref.5, f32[24,8,768]{2,1,0:T(8,128)S(1)} %copy-done.5, f32[24,8,768]{2,1,0:T(8,128)S(1)} %copy-done.3, f32[5,104,768]{2,1,0:T(8,128)S(1)} %subtract_dynamic-update-slice_fusion.coeff_ref), custom_call_target="tpu_custom_call" | custom-call | flops 92012544 | bytes 6291456 | tf_op jit(solution)/shard_map/pallas_call | solution.py:83
  61.8 4.4 all-to-all-done.refs_0_
  66.2 6.6 all-to-all-start.1
  72.8 1.6 fusion.5
  74.4 1.3 collective-permute-start.6
  75.7 5.5 collective-permute-start.5
  81.2 0.1 collective-permute-done.6.high_ref
  81.3 2.1 collective-permute-done.5.low_ref
  83.3 65.4 %shard_map.75 = (f32[64,40,512]{2,1,0:T(8,128)}, f32[64,40,256]{2,1,0:T(8,128)}) custom-call(f32[64,64,768]{2,1,0:T(8,128)} %x_ref.5, f32[40,8,768]{2,1,0:T(8,128)S(1)} %collective-permute-done.5.low_ref, f32[40,8,768]{2,1,0:T(8,128)S(1)} %collective-permute-done.6.high_ref, f32[5,104,768]{2,1,0:T(8,128)S(1)} %subtract_dynamic-update-slice_fusion.coeff_ref), custom_call_target="tpu_custom_call" | custom-call | flops 230031360 | bytes 15728640 | tf_op jit(solution)/shard_map/pallas_call | solution.py:83
  148.7 0.0 all-to-all-done.1.refs_1_
  148.7 5.8 all-to-all-start.4
  154.4 0.0 copy-done.11
  154.5 2.1 collective-permute-start
  156.6 74.0 %collective-permute-done = f32[1,2,128]{2,1,0:T(2,128)S(1)} collective-permute-done((f32[1,2,128]{2,1,0:T(2,128)S(1)}, f32[1,2,128]{2,1,0:T(2,128)S(1)}, u32[]{:S(2)}, u32[]{:S(2)}) %collective-permute-start) | collective-permute-done | bytes 1056 | tf_op jit(solution)/shard_map/ppermute | solution.py:332
  230.5 4.8 collective-permute-start.1
  235.4 26.6 %collective-permute-done.1 = f32[2,2,128]{2,1,0:T(2,128)S(1)} collective-permute-done((f32[2,2,128]{2,1,0:T(2,128)S(1)}, f32[2,2,128]{2,1,0:T(2,128)S(1)}, u32[]{:S(2)}, u32[]{:S(2)}) %collective-permute-start.1) | collective-permute-done | bytes 2080 | tf_op jit(solution)/shard_map/ppermute | solution.py:332
  262.0 1.5 collective-permute-start.2
  263.5 2.5 collective-permute-done.2
  266.0 0.0 all-to-all-done.4.refs_2_
  266.1 12.9 %all-to-all-start.2 = ((f32[8,8,40,256]{3,2,1,0:T(8,128)}), f32[8,8,40,256]{3,2,1,0:T(8,128)}, u32[]{:S(2)}, u32[]{:S(2)}) async-start(f32[8,8,40,256]{3,2,1,0:T(8,128)} %bitcast.23), calls=%async_computation.2 | async-start | bytes 5242880 | tf_op jit(solution)/shard_map/all_to_all | solution.py:341
  279.0 1.8 copy-done.1
  280.8 9.5 %shard_map.76 = f32[8,64,128]{2,1,0:T(8,128)S(1)} custom-call(s32[8,1,128]{2,1,0:T(1,128)S(1)} %get-tuple-element.34.cells_ref, f32[64,8,768]{2,1,0:T(8,128)S(1)} %copy-done, f32[64,16,768]{2,1,0:T(8,128)} %shard_map.74.refs_1_, f32[64,40,512]{2,1,0:T(8,128)} %get-tuple-element.11.refs_2_, f32[64,40,256]{2,1,0:T(8,128)S(1)} %copy-done.1), custom_call_target="tpu_custom_call" | custom-call | flops 2415919104 | bytes 12582912 | tf_op jit(solution)/shard_map/pallas_call | solution.py:134
  290.3 0.1 select_maximum_fusion
  290.3 0.1 constant_dynamic-slice_fusion
  290.4 0.0 copy-start.6
  290.4 2.1 collective-permute-start.7
  292.5 3.3 collective-permute-start.13
  295.9 0.1 collective-permute-start.12
  295.9 2.8 collective-permute-start.11
  298.8 0.6 collective-permute-start.10
  299.3 27.1 %collective-permute-done.7 = f32[1,64,384]{2,1,0:T(8,128)S(1)} collective-permute-done((f32[1,64,384]{2,1,0:T(8,128)S(1)}, f32[1,64,384]{2,1,0:T(8,128)S(1)}, u32[]{:S(2)}, u32[]{:S(2)}) %collective-permute-start.7) | collective-permute-done | bytes 98336 | tf_op jit(solution)/shard_map/ppermute | solution.py:351
  326.4 3.0 collective-permute-start.8
  329.4 21.4 %collective-permute-done.8 = f32[1,64,384]{2,1,0:T(8,128)S(1)} collective-permute-done((f32[1,64,384]{2,1,0:T(8,128)S(1)}, f32[1,64,384]{2,1,0:T(8,128)S(1)}, u32[]{:S(2)}, u32[]{:S(2)}) %collective-permute-start.8) | collective-permute-done | bytes 98336 | tf_op jit(solution)/shard_map/ppermute | solution.py:351
  350.8 1.8 collective-permute-start.9
  352.6 4.6 collective-permute-done.9
  357.3 0.0 collective-permute-done.10
  357.3 0.0 collective-permute-done.11
  357.3 0.0 collective-permute-done.12
  357.4 0.0 collective-permute-done.13
  357.6 14.7 %shard_map.77 = (bf16[512,512]{1,0:T(8,128)(2,1)S(1)}, bf16[512,512]{1,0:T(8,128)(2,1)S(1)}) custom-call(f32[8,64,384]{2,1,0:T(8,128)S(1)} %dynamic-slice_dynamic-update-slice_fusion.banks_ref, f32[1,384]{1,0:T(1,128)S(1)} %bitcast.24, f32[1,384]{1,0:T(1,128)S(1)} %bitcast.25), custom_call_target="tpu_custom_call" | custom-call | flops 16106127360 | bytes 1835008 | tf_op jit(solution)/shard_map/pallas_call | solution.py:231
  372.3 10.6 %shard_map.79 = f32[8,8,64,512]{3,2,1,0:T(8,128)} custom-call(bf16[512,512]{1,0:T(8,128)(2,1)S(1)} %get-tuple-element.13.mix_top_ref, bf16[512,512]{1,0:T(8,128)(2,1)S(1)} %get-tuple-element.14.mix_low_ref, f32[8,8,8,768]{3,2,1,0:T(8,128)S(1)} %all-to-all-done.refs_0_, f32[8,8,16,768]{3,2,1,0:T(8,128)} %all-to-all-done.1.refs_1_, ...), custom_call_target="tpu_custom_call" | custom-call | flops 6442450944 | bytes 16777216 | tf_op jit(solution)/shard_map/pallas_call | solution.py:281
  382.9 0.0 all-to-all-done.2.refs_2_
  382.9 5.0 all-to-all-start.5
  387.9 6.8 %shard_map.78 = f32[8,8,64,256]{3,2,1,0:T(8,128)} custom-call(bf16[512,512]{1,0:T(8,128)(2,1)S(1)} %get-tuple-element.13.mix_top_ref, bf16[512,512]{1,0:T(8,128)(2,1)S(1)} %get-tuple-element.14.mix_low_ref, f32[8,8,8,768]{3,2,1,0:T(8,128)S(1)} %all-to-all-done.refs_0_, f32[8,8,16,768]{3,2,1,0:T(8,128)} %all-to-all-done.1.refs_1_, ...), custom_call_target="tpu_custom_call" | custom-call | flops 3221225472 | bytes 8388608 | tf_op jit(solution)/shard_map/pallas_call | solution.py:281
  394.7 175.4 %all-to-all-done.5 = f32[8,8,64,512]{3,2,1,0:T(8,128)} async-done(((f32[8,8,64,512]{3,2,1,0:T(8,128)}), f32[8,8,64,512]{3,2,1,0:T(8,128)}, u32[]{:S(2)}, u32[]{:S(2)}) %all-to-all-start.5) | async-done | bytes 8388640 | tf_op jit(solution)/shard_map/all_to_all | solution.py:341
  570.1 4.6 all-to-all-start.3
  574.7 7.5 %shard_map.80.refs_0_ = f32[64,64,768]{2,1,0:T(8,128)} custom-call(f32[64,64,512]{2,1,0:T(8,128)} %bitcast.13.part_ref), custom_call_target="tpu_custom_call" | custom-call | bytes 16777216 | tf_op jit(solution)/shard_map/pallas_call | solution.py:304
  582.3 84.1 %all-to-all-done.3 = f32[8,8,64,256]{3,2,1,0:T(8,128)} async-done(((f32[8,8,64,256]{3,2,1,0:T(8,128)}), f32[8,8,64,256]{3,2,1,0:T(8,128)}, u32[]{:S(2)}, u32[]{:S(2)}) %all-to-all-start.3) | async-done | bytes 4194336 | tf_op jit(solution)/shard_map/all_to_all | solution.py:341
  666.4 5.0 shard_map.81
  (52 shorter events, 0.6 us)
Async XLA Ops:
  0.0 2.3 copy-start.7
  0.0 2.3 copy-start.8
  0.0 2.3 copy-start.9
  2.4 4.5 collective-permute-start.4
  3.7 4.8 collective-permute-start.3
  8.9 15.6 %copy-start.2 = (f32[24,8,768]{2,1,0:T(8,128)}, f32[24,8,768]{2,1,0:T(8,128)S(1)}, u32[]{:S(2)}) copy-start(f32[24,8,768]{2,1,0:T(8,128)S(1)} %slice.81.high_ref) | copy-start | bytes 1769476
  8.9 15.6 %copy-start.4 = (f32[24,8,768]{2,1,0:T(8,128)}, f32[24,8,768]{2,1,0:T(8,128)S(1)}, u32[]{:S(2)}) copy-start(f32[24,8,768]{2,1,0:T(8,128)S(1)} %slice.80.low_ref) | copy-start | bytes 1769476
  24.5 41.7 %all-to-all-start = ((f32[8,8,8,768]{3,2,1,0:T(8,128)}), f32[8,8,8,768]{3,2,1,0:T(8,128)S(1)}, u32[]{:S(2)}, u32[]{:S(2)}) async-start(f32[8,8,8,768]{3,2,1,0:T(8,128)} %bitcast.22), calls=%async_computation | async-start | bytes 3145728 | tf_op jit(solution)/shard_map/all_to_all | solution.py:341
  31.8 1.1 copy-start.3
  32.9 1.1 copy-start.5
  66.2 82.5 %all-to-all-start.1 = ((f32[8,8,16,768]{3,2,1,0:T(8,128)}), f32[8,8,16,768]{3,2,1,0:T(8,128)}, u32[]{:S(2)}, u32[]{:S(2)}) async-start(f32[8,8,16,768]{3,2,1,0:T(8,128)} %bitcast.26), calls=%async_computation.1 | async-start | bytes 6291456 | tf_op jit(solution)/shard_map/all_to_all | solution.py:341
  74.4 6.9 %collective-permute-start.6 = (f32[40,8,768]{2,1,0:T(8,128)S(1)}, f32[40,8,768]{2,1,0:T(8,128)S(1)}, u32[]{:S(2)}, u32[]{:S(2)}) collective-permute-start(f32[40,8,768]{2,1,0:T(8,128)S(1)} %get-tuple-element.15), channel_id=1, source_target_pairs={{4,0},{8,4},{12,8},{5,1},{9,5},{13,9},{6,2},{10,6},{14,10},{7,3},{... | collective-permute-start | bytes 2949128 | tf_op jit(solution)/shard_map/ppermute | solution.py:32
  75.7 7.6 %collective-permute-start.5 = (f32[40,8,768]{2,1,0:T(8,128)S(1)}, f32[40,8,768]{2,1,0:T(8,128)S(1)}, u32[]{:S(2)}, u32[]{:S(2)}) collective-permute-start(f32[40,8,768]{2,1,0:T(8,128)S(1)} %get-tuple-element.16), channel_id=1, source_target_pairs={{0,4},{4,8},{8,12},{1,5},{5,9},{9,13},{2,6},{6,10},{10,14},{3,7},{... | collective-permute-start | bytes 2949128 | tf_op jit(solution)/shard_map/ppermute | solution.py:32
  148.7 5.8 copy-start.11
  148.7 5.8 copy-start.10
  148.7 117.4 %all-to-all-start.4 = ((f32[8,8,40,512]{3,2,1,0:T(8,128)}), f32[8,8,40,512]{3,2,1,0:T(8,128)}, u32[]{:S(2)}, u32[]{:S(2)}) async-start(f32[8,8,40,512]{3,2,1,0:T(8,128)} %bitcast.27), calls=%async_computation.4 | async-start | bytes 10485760 | tf_op jit(solution)/shard_map/all_to_all | solution.py:341
  154.5 76.1 %collective-permute-start = (f32[1,2,128]{2,1,0:T(2,128)S(1)}, f32[1,2,128]{2,1,0:T(2,128)S(1)}, u32[]{:S(2)}, u32[]{:S(2)}) collective-permute-start(f32[1,2,128]{2,1,0:T(2,128)S(1)} %maximum_bitcast_fusion), channel_id=1, source_target_pairs={{0,1},{1,0},{2,3},{3,2},{16,17},{17,16},{18,19},{19,18},{4,5},{5,4... | collective-permute-start | bytes 3080 | tf_op jit(solution)/shard_map/ppermute | solution.py:332
  230.5 31.5 %collective-permute-start.1 = (f32[2,2,128]{2,1,0:T(2,128)S(1)}, f32[2,2,128]{2,1,0:T(2,128)S(1)}, u32[]{:S(2)}, u32[]{:S(2)}) collective-permute-start(f32[2,2,128]{2,1,0:T(2,128)S(1)} %maximum_select_fusion.2), channel_id=1, source_target_pairs={{0,2},{1,3},{2,0},{3,1},{16,18},{17,19},{18,16},{19,17},{4,6},{5,7... | collective-permute-start | bytes 6152 | tf_op jit(solution)/shard_map/ppermute | solution.py:332
  262.0 4.0 collective-permute-start.2
  266.1 12.9 %copy-start = (f32[64,8,768]{2,1,0:T(8,128)S(1)}, f32[64,8,768]{2,1,0:T(8,128)}, u32[]{:S(2)}) copy-start(f32[64,8,768]{2,1,0:T(8,128)} %shard_map.73.refs_0_) | copy-start | bytes 4718596
  266.1 116.8 %all-to-all-start.2 = ((f32[8,8,40,256]{3,2,1,0:T(8,128)}), f32[8,8,40,256]{3,2,1,0:T(8,128)}, u32[]{:S(2)}, u32[]{:S(2)}) async-start(f32[8,8,40,256]{3,2,1,0:T(8,128)} %bitcast.23), calls=%async_computation.2 | async-start | bytes 5242880 | tf_op jit(solution)/shard_map/all_to_all | solution.py:341
  279.0 1.8 copy-start.1
  290.4 67.2 %copy-start.6 = (f32[1,1,3,128]{3,1,2,0:T(1,128)S(1)}, f32[1,1,3,128]{3,1,2,0:T(1,128)}, u32[]{:S(2)}) copy-start(f32[1,1,3,128]{3,1,2,0:T(1,128)} %param.13) | copy-start | bytes 4612
  290.4 36.0 %collective-permute-start.7 = (f32[1,64,384]{2,1,0:T(8,128)S(1)}, f32[1,64,384]{2,1,0:T(8,128)S(1)}, u32[]{:S(2)}, u32[]{:S(2)}) collective-permute-start(f32[1,64,384]{2,1,0:T(8,128)S(1)} %get-tuple-element.27), channel_id=1, source_target_pairs={{0,1},{1,0},{2,3},{3,2},{16,17},{17,16},{18,19},{19,18},{4,5},{5,4... | collective-permute-start | bytes 294920 | tf_op jit(solution)/shard_map/ppermute | solution.py:351
  292.5 64.8 %collective-permute-start.13 = (f32[1,64,384]{2,1,0:T(8,128)S(1)}, f32[1,64,384]{2,1,0:T(8,128)S(1)}, u32[]{:S(2)}, u32[]{:S(2)}) collective-permute-start(f32[1,64,384]{2,1,0:T(8,128)S(1)} %get-tuple-element.21), channel_id=1, source_target_pairs={{0,19},{1,18},{2,17},{3,16},{16,3},{17,2},{18,1},{19,0},{4,23},{5,... | collective-permute-start | bytes 294920 | tf_op jit(solution)/shard_map/ppermute | solution.py:351
  295.9 61.5 %collective-permute-start.12 = (f32[1,64,384]{2,1,0:T(8,128)S(1)}, f32[1,64,384]{2,1,0:T(8,128)S(1)}, u32[]{:S(2)}, u32[]{:S(2)}) collective-permute-start(f32[1,64,384]{2,1,0:T(8,128)S(1)} %get-tuple-element.22), channel_id=1, source_target_pairs={{0,18},{1,19},{2,16},{3,17},{16,2},{17,3},{18,0},{19,1},{4,22},{5,... | collective-permute-start | bytes 294920 | tf_op jit(solution)/shard_map/ppermute | solution.py:351
  295.9 61.4 %collective-permute-start.11 = (f32[1,64,384]{2,1,0:T(8,128)S(1)}, f32[1,64,384]{2,1,0:T(8,128)S(1)}, u32[]{:S(2)}, u32[]{:S(2)}) collective-permute-start(f32[1,64,384]{2,1,0:T(8,128)S(1)} %get-tuple-element.23), channel_id=1, source_target_pairs={{0,17},{1,16},{2,19},{3,18},{16,1},{17,0},{18,3},{19,2},{4,21},{5,... | collective-permute-start | bytes 294920 | tf_op jit(solution)/shard_map/ppermute | solution.py:351
  298.8 58.5 %collective-permute-start.10 = (f32[1,64,384]{2,1,0:T(8,128)S(1)}, f32[1,64,384]{2,1,0:T(8,128)S(1)}, u32[]{:S(2)}, u32[]{:S(2)}) collective-permute-start(f32[1,64,384]{2,1,0:T(8,128)S(1)} %get-tuple-element.24), channel_id=1, source_target_pairs={{0,16},{1,17},{2,18},{3,19},{16,0},{17,1},{18,2},{19,3},{4,20},{5,... | collective-permute-start | bytes 294920 | tf_op jit(solution)/shard_map/ppermute | solution.py:351
  326.4 24.4 %collective-permute-start.8 = (f32[1,64,384]{2,1,0:T(8,128)S(1)}, f32[1,64,384]{2,1,0:T(8,128)S(1)}, u32[]{:S(2)}, u32[]{:S(2)}) collective-permute-start(f32[1,64,384]{2,1,0:T(8,128)S(1)} %get-tuple-element.26), channel_id=1, source_target_pairs={{0,2},{1,3},{2,0},{3,1},{16,18},{17,19},{18,16},{19,17},{4,6},{5,7... | collective-permute-start | bytes 294920 | tf_op jit(solution)/shard_map/ppermute | solution.py:351
  350.8 6.4 collective-permute-start.9
  382.9 187.2 %all-to-all-start.5 = ((f32[8,8,64,512]{3,2,1,0:T(8,128)}), f32[8,8,64,512]{3,2,1,0:T(8,128)}, u32[]{:S(2)}, u32[]{:S(2)}) async-start(f32[8,8,64,512]{3,2,1,0:T(8,128)} %shard_map.79), calls=%async_computation.5 | async-start | bytes 16777216 | tf_op jit(solution)/shard_map/all_to_all | solution.py:341
  570.1 96.2 %all-to-all-start.3 = ((f32[8,8,64,256]{3,2,1,0:T(8,128)}), f32[8,8,64,256]{3,2,1,0:T(8,128)}, u32[]{:S(2)}, u32[]{:S(2)}) async-start(f32[8,8,64,256]{3,2,1,0:T(8,128)} %shard_map.78), calls=%async_computation.3 | async-start | bytes 8388608 | tf_op jit(solution)/shard_map/all_to_all | solution.py:341

commit v3 on v2

--- a/solution.py
+++ b/solution.py
@@ -143,15 +143,21 @@
     )(cells, *flat)
 
 
-def mixing_body(layout, banks_ref, values_ref, weights_ref, top_ref, low_ref, *scratch):
-    stacked_ref, weighted_ref, one_ref, two_ref, factor_ref, inverse_ref = scratch
-    sources = banks_ref.shape[0]
+def mixing_body(layout, me_ref, *refs):
+    banks, refs = refs[:-10], refs[-10:]
+    values_ref, weights_ref, top_ref, low_ref = refs[:4]
+    stacked_ref, weighted_ref, one_ref, two_ref, factor_ref, inverse_ref = refs[4:]
     size, wide = stacked_ref.shape
-    at, start = 0, 0
+    sources = sum(ref.shape[0] for ref in banks)
+    start = 0
     for _, count in layout:
-        for source in range(sources):
-            stacked_ref[at : at + count] = banks_ref[source, start : start + count, :]
-            at += count
+        for step in range(sources):
+            if len(banks) == 1:
+                source, piece = step, banks[0].at[step]
+            else:
+                source, piece = me_ref[0] ^ step, banks[step].at[0]
+            at = pl.multiple_of(start * sources + source * count, 8)
+            stacked_ref[pl.ds(at, count), :] = piece[start : start + count, :]
         start += count
     bank = stacked_ref[...]
     mean = jnp.sum(bank, axis=0, keepdims=True) / size
@@ -225,16 +231,18 @@
 
 
 def mixing_matrix(banks, values, weights, layout):
-    sources, count, wide = banks.shape
-    size = sources * count
+    _, count, wide = banks[0].shape
+    size = sum(bank.shape[0] for bank in banks) * count
+    whole = pl.BlockSpec(memory_space=pltpu.VMEM)
     out = jax.ShapeDtypeStruct((size, size), BF16)
     return call(
         functools.partial(mixing_body, layout),
         flops=6 * 2 * 10 * size * size * size,
         moved=4 * size * (wide + size),
+        in_specs=[pl.BlockSpec(memory_space=pltpu.SMEM)] + [whole] * (len(banks) + 2),
         out_shape=(out, out),
         scratch_shapes=[pltpu.VMEM((size, wide), F32)] * 2 + [pltpu.VMEM((size, size), F32)] * 4,
-    )(banks, values, weights)
+    )(lax.axis_index(GROUP).reshape(1), *banks, values, weights)
 
 
 def analyse_body(layout, mix_top_ref, mix_low_ref, *refs):
@@ -268,6 +276,7 @@
 
 
 def analyse(mix_top, mix_low, chunks, layout, lanes):
+    tile = lanes if all(first % lanes == 0 for _, first in chunks) else LANES
     sources, block_rows, _, _ = chunks[0][0].shape
     count = sum(chunk.shape[2] for chunk, _ in chunks)
     size = sources * count
@@ -275,17 +284,17 @@
 
     def spec(chunk, first):
         return pl.BlockSpec(
-            (sources, step, chunk.shape[2], lanes), lambda r: (0, r, 0, first // lanes)
+            (sources, step, chunk.shape[2], tile), lambda r, t: (0, r, 0, first // tile + t)
         )
 
     return call(
         functools.partial(analyse_body, layout),
         flops=6 * size * size * block_rows * lanes,
         moved=8 * size * block_rows * lanes,
-        grid=(block_rows // step,),
-        in_specs=[pl.BlockSpec((size, size), lambda r: (0, 0))] * 2
+        grid=(block_rows // step, lanes // tile),
+        in_specs=[pl.BlockSpec((size, size), lambda r, t: (0, 0))] * 2
         + [spec(chunk, first) for chunk, first in chunks],
-        out_specs=pl.BlockSpec((sources, step, count, lanes), lambda r: (0, r, 0, 0)),
+        out_specs=pl.BlockSpec((sources, step, count, tile), lambda r, t: (0, r, 0, t)),
         out_shape=pltpu.HBM((sources, block_rows, count, lanes), F32),
     )(mix_top, mix_low, *[chunk for chunk, _ in chunks])
 
@@ -299,19 +308,48 @@
 
 def place(part, whole, first, lon):
     rows, count, lanes = part.shape
-    group = 16 if count % 16 == 0 else 8
+    group, tile = 8, lanes if first % lanes == 0 else LANES
     out = jax.ShapeDtypeStruct((count, rows, lon), F32)
     return call(
         place_body,
         flops=0,
         moved=8 * rows * count * lanes,
-        grid=(count // group,),
-        in_specs=[pl.BlockSpec((rows, group, lanes), lambda i: (0, i, 0))]
+        grid=(count // group, lanes // tile),
+        in_specs=[pl.BlockSpec((rows, group, tile), lambda i, t: (0, i, t))]
         + ([] if whole is None else [pl.BlockSpec(memory_space=pl.ANY)]),
-        out_specs=pl.BlockSpec((group, rows, lanes), lambda i: (i, 0, first // lanes)),
+        out_specs=pl.BlockSpec((group, rows, tile), lambda i, t: (i, 0, first // tile + t)),
         out_shape=out,
         input_output_aliases={} if whole is None else {1: 0},
     )(*((part,) if whole is None else (part, whole)))
+
+
+def place_steps_body(me_ref, *refs):
+    out_ref = refs[-1]
+    for step, ref in enumerate(refs[:-1]):
+        if len(ref.shape) == 4:
+            rows = ref.shape[1]
+            at = pl.multiple_of((me_ref[0] ^ step) * rows, rows)
+            out_ref[:, pl.ds(at, rows), :] = jnp.swapaxes(ref[0], 0, 1)
+
+
+def place_steps(pieces, whole, first, lon):
+    _, block_rows, count, lanes = pieces[0].shape
+    rows, group = len(pieces) * block_rows, 8
+    spec = pl.BlockSpec((1, block_rows, group, lanes), lambda i, me: (0, 0, i, 0))
+    return call(
+        place_steps_body,
+        flops=0,
+        moved=8 * rows * count * lanes,
+        grid_spec=pltpu.PrefetchScalarGridSpec(
+            num_scalar_prefetch=1,
+            grid=(count // group,),
+            in_specs=[spec] * len(pieces)
+            + ([] if whole is None else [pl.BlockSpec(memory_space=pl.ANY)]),
+            out_specs=pl.BlockSpec((group, rows, lanes), lambda i, me: (i, 0, first // lanes)),
+        ),
+        out_shape=jax.ShapeDtypeStruct((count, rows, lon), F32),
+        input_output_aliases={} if whole is None else {1 + len(pieces): 0},
+    )(lax.axis_index(GROUP).reshape(1), *pieces, *([] if whole is None else [whole]))
 
 
 def member_chunks(count):
@@ -323,6 +361,17 @@
 def lane_parts(lon):
     third = lon // 3
     return (2 * third, third) if lon % (3 * LANES) == 0 else (lon,)
+
+
+def return_parts(lon, block_rows):
+    if lon == 6 * LANES and block_rows % 8 == 0:
+        third = 2 * LANES
+        return (
+            ((third + LANES, LANES, True), (0, third + LANES, False)),
+            ((2 * third, LANES, True), (2 * third + LANES, LANES, False)),
+        )
+    parts = lane_parts(lon)
+    return tuple(((sum(parts[:j]), lanes, False),) for j, lanes in enumerate(parts))
 
 
 def gathered(row):
@@ -344,13 +393,12 @@
 def exchange_by_steps(array):
     size, me = array.shape[0], lax.axis_index(GROUP)
     if size > 8 or size & (size - 1):
-        return exchange(array)
+        return [exchange(array)]
     pieces = [lax.dynamic_slice_in_dim(array, me, 1)]
     for step in range(1, size):
         piece = lax.dynamic_slice_in_dim(array, me ^ step, 1)
         pieces.append(lax.ppermute(piece, GROUP, [(i, i ^ step) for i in range(size)]))
-    pieces = jnp.concatenate(pieces)
-    return jnp.concatenate([lax.dynamic_slice_in_dim(pieces, me ^ i, 1) for i in range(size)])
+    return pieces
 
 
 def on_device(starting_states, courant_x, courant_y, diffusion, obs_index, obs_value, loc_weight):
@@ -416,13 +464,20 @@
     values = lax.dynamic_slice_in_dim(values, lax.axis_index(GROUP), 3).reshape(1, 3 * obs)
     mix_top, mix_low = mixing_matrix(banks, values, loc_weight.reshape(1, 3 * obs), layout)
 
-    result, first = None, 0
-    for j, lanes in enumerate(widths):
-        chunks = [(chunk[0], first) if len(chunk) == 1 else (chunk[j], 0) for chunk in received]
-        part = analyse(mix_top, mix_low, chunks, layout, lanes)
-        part = exchange(part)
-        result = place(part.reshape(rows, members, lanes), result, first, lon)
-        first += lanes
+    result = None
+    for j, pieces in enumerate(return_parts(lon, block_rows)):
+        base = sum(widths[:j])
+        for first, lanes, stepwise in pieces:
+            chunks = [
+                (chunk[0], first) if len(chunk) == 1 else (chunk[j], first - base) for chunk in received
+            ]
+            part = analyse(mix_top, mix_low, chunks, layout, lanes)
+            part = exchange_by_steps(part) if stepwise else exchange(part)
+            if stepwise and len(part) > 1:
+                result = place_steps(part, result, first, lon)
+            else:
+                part = part[0] if stepwise else part
+                result = place(part.reshape(rows, members, lanes), result, first, lon)
     return result
 
 

time: 673 us -> 697 us (1.036)
  waiting for transfers between devices: 424 us -> 290 us
  blocking collectives: 0 us -> 119 us
  starting transfers between devices: 75.3 us -> 89.7 us
  Pallas kernels: 163 us -> 177 us
  local copies, waits for them, and re-layouts: 8.31 us -> 16.7 us
    all_to_all x6 -> x5, waiting for transfers between devices: 264 us -> 138 us  [exchange(): return lax.all_to_all(array, GROUP, split_axis=0, concat_axis=0, tiled=True)]
    all_to_all x0 -> x1, blocking collectives: none -> 119 us  [exchange(): return lax.all_to_all(array, GROUP, split_axis=0, concat_axis=0, tiled=True)]
    ppermute x3, waiting for transfers between devices: 103 us -> 53.3 us  [gathered(): other = lax.ppermute(row, GROUP, [(i, i ^ bit) for i in range(size)])]
    ppermute x7 -> x21, waiting for transfers between devices: 53.2 us -> 94.7 us  [exchange_by_steps(): lax.ppermute(piece, GROUP, [(i, i ^ step) for i in range(size)])]
    ppermute x7 -> x21, starting transfers between devices: 13.6 us -> 43.4 us  [exchange_by_steps(): lax.ppermute(piece, GROUP, [(i, i ^ step) for i in range(size)])]
    all_to_all x6 -> x5, starting transfers between devices: 42.2 us -> 28.1 us  [exchange(): return lax.all_to_all(array, GROUP, split_axis=0, concat_axis=0, tiled=True)]
    pallas_call x2 -> x4, Pallas kernels: 17.4 us -> 23.4 us  [analyse(): call(functools.partial(analyse_body, layout), flops=6 * size * size * blo...]
  transfers between devices with their start and end apart: 20 -> 33, of which waited for: 12 -> 19; matrix products, arithmetic and copies ran while one was open for 0% -> 1% of each run, Pallas kernels for 21% -> 22%
where the time goes in v3:
time: 697 us; the launch traced here: 694 us
  waiting for transfers between devices  290 us (42%)
  Pallas kernels  177 us (25%)
  blocking collectives  119 us (17%)
  starting transfers between devices  89.7 us (13%)
  local copies, waits for them, and re-layouts  16.7 us (2%)
    all_to_all x5, waiting for transfers between devices, exchange(): return lax.all_to_all(array, GROUP, split_axis=0, concat_axis=0, tiled=True)  138 us
    all_to_all x1, blocking collectives, exchange(): return lax.all_to_all(array, GROUP, split_axis=0, concat_axis=0, tiled=True)  119 us
    pallas_call x3, Pallas kernels, forecast(): call(forecast_body, flops=9 * FSTEPS * total * count * lon, moved=8 * cou...  109 us
    ppermute x21, waiting for transfers between devices, exchange_by_steps(): lax.ppermute(piece, GROUP, [(i, i ^ step) for i in range(size)])  94.7 us
    ppermute x3, waiting for transfers between devices, gathered(): other = lax.ppermute(row, GROUP, [(i, i ^ bit) for i in range(size)])  53.3 us
    ppermute x21, starting transfers between devices, exchange_by_steps(): lax.ppermute(piece, GROUP, [(i, i ^ step) for i in range(size)])  43.4 us
    all_to_all x5, starting transfers between devices, exchange(): return lax.all_to_all(array, GROUP, split_axis=0, concat_axis=0, tiled=True)  28.1 us
    pallas_call x4, Pallas kernels, analyse(): call(functools.partial(analyse_body, layout), flops=6 * size * size * blo...  23.4 us
  transfers between devices with their start and end apart: 33, of which 19 were waited for; matrix products, arithmetic and copies ran while one was open for 1% of the time, Pallas kernels for 22%

profile of v3, /device:TPU:0, one launch (start us, length us, event | category | flops | bytes accessed | tf_op | source)
XLA Modules:
  0.0 694.3 jit_solution(5197087925981432970)
XLA Ops:
  0.0 1.1 fusion.6
  1.1 1.2 fusion.7
  2.4 1.3 collective-permute-start.4
  3.7 3.1 collective-permute-start.3
  6.9 1.6 collective-permute-done.3
  9.0 16.0 %shard_map.73.refs_0_ = f32[64,8,768]{2,1,0:T(8,128)} custom-call(f32[64,64,768]{2,1,0:T(8,128)} %x_ref.5, f32[24,8,768]{2,1,0:T(8,128)S(1)} %slice.80.low_ref, f32[24,8,768]{2,1,0:T(8,128)S(1)} %slice.81.high_ref, f32[5,104,768]{2,1,0:T(8,128)S(1)} %subtract_dynamic-update-slice_fusion.coeff_ref), custom_call_target="tpu_custom_call" | custom-call | flops 46006272 | bytes 3145728 | tf_op jit(solution)/shard_map/pallas_call | solution.py:83
  25.0 7.3 %all-to-all-start = ((f32[8,8,8,768]{3,2,1,0:T(8,128)}), f32[8,8,8,768]{3,2,1,0:T(8,128)S(1)}, u32[]{:S(2)}, u32[]{:S(2)}) async-start(f32[8,8,8,768]{3,2,1,0:T(8,128)} %bitcast.23), calls=%async_computation | async-start | bytes 3145728 | tf_op jit(solution)/shard_map/all_to_all | solution.py:390
  33.3 1.1 copy-done.12
  34.4 27.8 %shard_map.74.refs_1_ = f32[64,16,768]{2,1,0:T(8,128)} custom-call(f32[64,64,768]{2,1,0:T(8,128)} %x_ref.5, f32[24,8,768]{2,1,0:T(8,128)S(1)} %copy-done.12, f32[24,8,768]{2,1,0:T(8,128)S(1)} %copy-done.10, f32[5,104,768]{2,1,0:T(8,128)S(1)} %subtract_dynamic-update-slice_fusion.coeff_ref), custom_call_target="tpu_custom_call" | custom-call | flops 92012544 | bytes 6291456 | tf_op jit(solution)/shard_map/pallas_call | solution.py:83
  62.2 4.4 all-to-all-done.refs_0_
  66.6 1.2 copy-done.2
  67.8 6.6 all-to-all-start.1
  74.4 1.8 fusion.5
  76.1 1.3 collective-permute-start.6
  77.4 4.7 collective-permute-start.5
  82.2 2.1 collective-permute-done.5.low_ref
  84.2 65.4 %shard_map.75 = (f32[64,40,512]{2,1,0:T(8,128)}, f32[64,40,256]{2,1,0:T(8,128)}) custom-call(f32[64,64,768]{2,1,0:T(8,128)} %x_ref.5, f32[40,8,768]{2,1,0:T(8,128)S(1)} %collective-permute-done.5.low_ref, f32[40,8,768]{2,1,0:T(8,128)S(1)} %collective-permute-done.6.high_ref, f32[5,104,768]{2,1,0:T(8,128)S(1)} %copy-done.6), custom_call_target="tpu_custom_call" | custom-call | flops 230031360 | bytes 15728640 | tf_op jit(solution)/shard_map/pallas_call | solution.py:83
  149.6 119.4 %all_to_all.30.refs_2_ = f32[8,8,40,512]{3,2,1,0:T(8,128)} all-to-all(f32[8,8,40,512]{3,2,1,0:T(8,128)} %bitcast.28), channel_id=1, replica_groups=mesh['members'=2,'lat'=4,'blk'=4] {'members','blk'}, dimensions={0} | all-to-all | bytes 10485760 | tf_op jit(solution)/shard_map/all_to_all | solution.py:390
  269.0 4.7 all-to-all-start.2
  273.8 1.8 collective-permute-start
  275.6 38.2 %collective-permute-done = f32[1,2,128]{2,1,0:T(2,128)S(1)} collective-permute-done((f32[1,2,128]{2,1,0:T(2,128)S(1)}, f32[1,2,128]{2,1,0:T(2,128)S(1)}, u32[]{:S(2)}, u32[]{:S(2)}) %collective-permute-start) | collective-permute-done | bytes 1056 | tf_op jit(solution)/shard_map/ppermute | solution.py:381
  313.7 4.6 collective-permute-start.1
  318.4 12.6 %collective-permute-done.1 = f32[2,2,128]{2,1,0:T(2,128)S(1)} collective-permute-done((f32[2,2,128]{2,1,0:T(2,128)S(1)}, f32[2,2,128]{2,1,0:T(2,128)S(1)}, u32[]{:S(2)}, u32[]{:S(2)}) %collective-permute-start.1) | collective-permute-done | bytes 2080 | tf_op jit(solution)/shard_map/ppermute | solution.py:381
  331.0 1.5 collective-permute-start.2
  332.5 2.5 collective-permute-done.2
  335.0 1.4 copy-done.7
  336.4 1.7 copy-done.8
  338.1 9.5 %shard_map.76 = f32[8,64,128]{2,1,0:T(8,128)S(1)} custom-call(s32[8,1,128]{2,1,0:T(1,128)S(1)} %get-tuple-element.50.cells_ref, f32[64,8,768]{2,1,0:T(8,128)S(1)} %copy-done.7, f32[64,16,768]{2,1,0:T(8,128)} %shard_map.74.refs_1_, f32[64,40,512]{2,1,0:T(8,128)} %get-tuple-element.11.refs_2_, f32[64,40,256]{2,1,0:T(8,128)S(1)} %copy-done.8), custom_call_target="tpu_custom_call" | custom-call | flops 2415919104 | bytes 12582912 | tf_op jit(solution)/shard_map/pallas_call | solution.py:134
  348.6 5.4 collective-permute-start.13
  354.4 1.6 collective-permute-start.10
  356.0 3.5 collective-permute-start.9
  360.1 2.8 collective-permute-done.12.refs_6_
  362.9 1.3 collective-permute-done.10.refs_4_
  364.8 5.5 collective-permute-done.8.refs_2_
  370.3 14.8 %shard_map.77 = (bf16[512,512]{1,0:T(8,128)(2,1)S(1)}, bf16[512,512]{1,0:T(8,128)(2,1)S(1)}) custom-call(s32[1]{0:T(128)} %bitcast.me_ref, f32[1,64,384]{2,1,0:T(8,128)S(1)} %get-tuple-element.44.refs_0_, f32[1,64,384]{2,1,0:T(8,128)S(1)} %collective-permute-done.7.refs_1_, f32[1,64,384]{2,1,0:T(8,128)S(1)} %collective-permute-done.8.refs_2_, ...), custom_call_target="tpu_custom_call" | custom-call | flops 16106127360 | bytes 1835008 | tf_op jit(solution)/shard_map/pallas_call | solution.py:238
  385.1 8.7 %shard_map.80 = f32[8,8,64,384]{3,2,1,0:T(8,128)} custom-call(bf16[512,512]{1,0:T(8,128)(2,1)S(1)} %get-tuple-element.13.mix_top_ref, bf16[512,512]{1,0:T(8,128)(2,1)S(1)} %get-tuple-element.14.mix_low_ref, f32[8,8,8,768]{3,2,1,0:T(8,128)S(1)} %copy-done.3, f32[8,8,16,768]{3,2,1,0:T(8,128)S(1)} %all-to-all-done.1.refs_1_, f32[8,8,40,512]{3,2,1,0:T(8,128)} %all_to_all.30.refs_2_), custom_call_target="tpu_custom_call" | custom-call | flops 4831838208 | bytes 12582912 | tf_op jit(solution)/shard_map/pallas_call | solution.py:290
  395.4 4.9 all-to-all-start.5
  400.3 5.0 shard_map.78
  405.3 134.0 %all-to-all-done.5 = f32[8,8,64,384]{3,2,1,0:T(8,128)} async-done(((f32[8,8,64,384]{3,2,1,0:T(8,128)}), f32[8,8,64,384]{3,2,1,0:T(8,128)}, u32[]{:S(2)}, u32[]{:S(2)}) %all-to-all-start.5) | async-done | bytes 6291488 | tf_op jit(solution)/shard_map/all_to_all | solution.py:390
  539.3 4.6 all-to-all-start.3
  543.9 5.0 shard_map.79
  548.9 1.9 constant_dynamic-slice_fusion.8
  550.8 4.5 collective-permute-start.20
  555.2 4.8 shard_map.81
  560.0 1.7 constant_dynamic-slice_fusion
  561.8 3.0 collective-permute-start.27
  565.7 1.9 collective-permute-start.25
  567.7 21.9 %collective-permute-done.20.refs_7_ = f32[1,8,64,128]{3,2,1,0:T(8,128)S(1)} collective-permute-done((f32[1,8,64,128]{3,2,1,0:T(8,128)S(1)}, f32[1,8,64,128]{3,2,1,0:T(8,128)S(1)}, u32[]{:S(2)}, u32[]{:S(2)}) %collective-permute-start.20) | collective-permute-done | bytes 262176 | tf_op jit(solution)/shard_map/ppermute | solution.py:400
  590.1 39.1 %collective-permute-done.19.refs_6_ = f32[1,8,64,128]{3,2,1,0:T(8,128)S(1)} collective-permute-done((f32[1,8,64,128]{3,2,1,0:T(8,128)S(1)}, f32[1,8,64,128]{3,2,1,0:T(8,128)S(1)}, u32[]{:S(2)}, u32[]{:S(2)}) %collective-permute-start.19) | collective-permute-done | bytes 262176 | tf_op jit(solution)/shard_map/ppermute | solution.py:400
  629.2 3.0 collective-permute-start.23
  632.2 10.4 %collective-permute-start.22 = (f32[1,8,64,128]{3,2,1,0:T(8,128)S(1)}, f32[1,8,64,128]{3,2,1,0:T(8,128)S(1)}, u32[]{:S(2)}, u32[]{:S(2)}) collective-permute-start(f32[1,8,64,128]{3,2,1,0:T(8,128)S(1)} %get-tuple-element.26), channel_id=1, source_target_pairs={{0,2},{1,3},{2,0},{3,1},{16,18},{17,19},{18,16},{19,17},{4,6},{5,7... | collective-permute-start | bytes 786440 | tf_op jit(solution)/shard_map/ppermute | solution.py:400
  642.6 9.1 %collective-permute-done.26.refs_6_ = f32[1,8,64,128]{3,2,1,0:T(8,128)S(1)} collective-permute-done((f32[1,8,64,128]{3,2,1,0:T(8,128)S(1)}, f32[1,8,64,128]{3,2,1,0:T(8,128)S(1)}, u32[]{:S(2)}, u32[]{:S(2)}) %collective-permute-start.26) | collective-permute-done | bytes 262176 | tf_op jit(solution)/shard_map/ppermute | solution.py:400
  651.7 1.7 collective-permute-start.18
  653.3 1.8 collective-permute-start.17
  655.1 3.1 collective-permute-start.16
  658.2 1.1 collective-permute-done.22.refs_2_
  659.3 5.4 collective-permute-done.21.refs_1_
  664.8 1.1 collective-permute-start.14
  665.9 3.3 shard_map.82.refs_0_
  669.2 8.0 %shard_map.83.refs_8_ = f32[64,64,768]{2,1,0:T(8,128)} custom-call(f32[64,64,384]{2,1,0:T(8,128)} %bitcast.14.part_ref, f32[64,64,768]{2,1,0:T(8,128)} %shard_map.82.refs_0_), custom_call_target="tpu_custom_call", output_to_operand_aliasing={{}: (1, {})} | custom-call | bytes 12582912 | tf_op jit(solution)/shard_map/pallas_call | solution.py:313
  677.3 4.6 collective-permute-done.15.refs_2_
  681.9 3.3 collective-permute-done.14.refs_1_
  685.2 3.3 shard_map.84.refs_0_
  688.5 5.7 shard_map.85
  (92 shorter events, 7.5 us)
Async XLA Ops:
  0.0 2.3 copy-start.18
  0.0 2.3 copy-start.19
  0.0 2.3 copy-start.20
  2.4 4.5 collective-permute-start.4
  3.7 4.8 collective-permute-start.3
  8.8 23.4 %copy-start.5 = (f32[5,104,768]{2,1,0:T(8,128)}, f32[5,104,768]{2,1,0:T(8,128)S(1)}, u32[]{:S(2)}) copy-start(f32[5,104,768]{2,1,0:T(8,128)S(1)} %subtract_dynamic-update-slice_fusion.coeff_ref) | copy-start | bytes 4792324
  8.9 16.0 %copy-start.9 = (f32[24,8,768]{2,1,0:T(8,128)}, f32[24,8,768]{2,1,0:T(8,128)S(1)}, u32[]{:S(2)}) copy-start(f32[24,8,768]{2,1,0:T(8,128)S(1)} %slice.81.high_ref) | copy-start | bytes 1769476
  9.0 16.0 %copy-start.11 = (f32[24,8,768]{2,1,0:T(8,128)}, f32[24,8,768]{2,1,0:T(8,128)S(1)}, u32[]{:S(2)}) copy-start(f32[24,8,768]{2,1,0:T(8,128)S(1)} %slice.80.low_ref) | copy-start | bytes 1769476
  25.0 41.7 %all-to-all-start = ((f32[8,8,8,768]{3,2,1,0:T(8,128)}), f32[8,8,8,768]{3,2,1,0:T(8,128)S(1)}, u32[]{:S(2)}, u32[]{:S(2)}) async-start(f32[8,8,8,768]{3,2,1,0:T(8,128)} %bitcast.23), calls=%async_computation | async-start | bytes 3145728 | tf_op jit(solution)/shard_map/all_to_all | solution.py:390
  32.3 1.1 copy-start.10
  33.3 1.1 copy-start.12
  66.6 1.2 copy-start.2
  67.8 81.9 %all-to-all-start.1 = ((f32[8,8,16,768]{3,2,1,0:T(8,128)}), f32[8,8,16,768]{3,2,1,0:T(8,128)S(1)}, u32[]{:S(2)}, u32[]{:S(2)}) async-start(f32[8,8,16,768]{3,2,1,0:T(8,128)} %bitcast.27), calls=%async_computation.1 | async-start | bytes 6291456 | tf_op jit(solution)/shard_map/all_to_all | solution.py:390
  74.4 9.9 %copy-start.6 = (f32[5,104,768]{2,1,0:T(8,128)S(1)}, f32[5,104,768]{2,1,0:T(8,128)}, u32[]{:S(2)}) copy-start(f32[5,104,768]{2,1,0:T(8,128)} %copy-done.5) | copy-start | bytes 4792324
  76.1 6.0 collective-permute-start.6
  77.4 6.8 collective-permute-start.5
  149.6 235.5 %copy-start = (f32[8,8,16,768]{3,2,1,0:T(8,128)}, f32[8,8,16,768]{3,2,1,0:T(8,128)S(1)}, u32[]{:S(2)}) copy-start(f32[8,8,16,768]{3,2,1,0:T(8,128)S(1)} %all-to-all-done.1.refs_1_) | copy-start | bytes 9437188
  269.0 4.7 copy-start.22
  269.0 4.7 copy-start.21
  269.0 126.3 %all-to-all-start.2 = ((f32[8,8,40,256]{3,2,1,0:T(8,128)}), f32[8,8,40,256]{3,2,1,0:T(8,128)}, u32[]{:S(2)}, u32[]{:S(2)}) async-start(f32[8,8,40,256]{3,2,1,0:T(8,128)} %bitcast.24), calls=%async_computation.2 | async-start | bytes 5242880 | tf_op jit(solution)/shard_map/all_to_all | solution.py:390
  273.8 39.9 %collective-permute-start = (f32[1,2,128]{2,1,0:T(2,128)S(1)}, f32[1,2,128]{2,1,0:T(2,128)S(1)}, u32[]{:S(2)}, u32[]{:S(2)}) collective-permute-start(f32[1,2,128]{2,1,0:T(2,128)S(1)} %maximum_bitcast_fusion), channel_id=1, source_target_pairs={{0,1},{1,0},{2,3},{3,2},{16,17},{17,16},{18,19},{19,18},{4,5},{5,4... | collective-permute-start | bytes 3080 | tf_op jit(solution)/shard_map/ppermute | solution.py:381
  313.7 17.2 %collective-permute-start.1 = (f32[2,2,128]{2,1,0:T(2,128)S(1)}, f32[2,2,128]{2,1,0:T(2,128)S(1)}, u32[]{:S(2)}, u32[]{:S(2)}) collective-permute-start(f32[2,2,128]{2,1,0:T(2,128)S(1)} %maximum_select_fusion.2), channel_id=1, source_target_pairs={{0,2},{1,3},{2,0},{3,1},{16,18},{17,19},{18,16},{19,17},{4,6},{5,7... | collective-permute-start | bytes 6152 | tf_op jit(solution)/shard_map/ppermute | solution.py:381
  331.0 4.0 collective-permute-start.2
  335.0 1.4 copy-start.7
  336.4 1.7 copy-start.8
  347.7 22.6 %copy-start.17 = (f32[1,1,3,128]{3,1,2,0:T(1,128)S(1)}, f32[1,1,3,128]{3,1,2,0:T(1,128)}, u32[]{:S(2)}) copy-start(f32[1,1,3,128]{3,1,2,0:T(1,128)} %param.13) | copy-start | bytes 4612
  348.6 10.9 %collective-permute-start.13 = (f32[1,64,384]{2,1,0:T(8,128)}, f32[1,64,384]{2,1,0:T(8,128)S(1)}, u32[]{:S(2)}, u32[]{:S(2)}) collective-permute-start(f32[1,64,384]{2,1,0:T(8,128)} %get-tuple-element.37), channel_id=1, source_target_pairs={{0,19},{1,18},{2,17},{3,16},{16,3},{17,2},{18,1},{19,0},{4,23},{5,... | collective-permute-start | bytes 294920 | tf_op jit(solution)/shard_map/ppermute | solution.py:400
  354.0 8.8 %collective-permute-start.12 = (f32[1,64,384]{2,1,0:T(8,128)}, f32[1,64,384]{2,1,0:T(8,128)S(1)}, u32[]{:S(2)}, u32[]{:S(2)}) collective-permute-start(f32[1,64,384]{2,1,0:T(8,128)} %get-tuple-element.38), channel_id=1, source_target_pairs={{0,18},{1,19},{2,16},{3,17},{16,2},{17,3},{18,0},{19,1},{4,22},{5,... | collective-permute-start | bytes 294920 | tf_op jit(solution)/shard_map/ppermute | solution.py:400
  354.0 8.9 %collective-permute-start.11 = (f32[1,64,384]{2,1,0:T(8,128)}, f32[1,64,384]{2,1,0:T(8,128)S(1)}, u32[]{:S(2)}, u32[]{:S(2)}) collective-permute-start(f32[1,64,384]{2,1,0:T(8,128)} %get-tuple-element.39), channel_id=1, source_target_pairs={{0,17},{1,16},{2,19},{3,18},{16,1},{17,0},{18,3},{19,2},{4,21},{5,... | collective-permute-start | bytes 294920 | tf_op jit(solution)/shard_map/ppermute | solution.py:400
  354.4 9.7 %collective-permute-start.10 = (f32[1,64,384]{2,1,0:T(8,128)}, f32[1,64,384]{2,1,0:T(8,128)S(1)}, u32[]{:S(2)}, u32[]{:S(2)}) collective-permute-start(f32[1,64,384]{2,1,0:T(8,128)} %get-tuple-element.40), channel_id=1, source_target_pairs={{0,16},{1,17},{2,18},{3,19},{16,0},{17,1},{18,2},{19,3},{4,20},{5,... | collective-permute-start | bytes 294920 | tf_op jit(solution)/shard_map/ppermute | solution.py:400
  356.0 8.8 %collective-permute-start.9 = (f32[1,64,384]{2,1,0:T(8,128)}, f32[1,64,384]{2,1,0:T(8,128)S(1)}, u32[]{:S(2)}, u32[]{:S(2)}) collective-permute-start(f32[1,64,384]{2,1,0:T(8,128)} %get-tuple-element.41), channel_id=1, source_target_pairs={{0,3},{1,2},{2,1},{3,0},{16,19},{17,18},{18,17},{19,16},{4,7},{5,6... | collective-permute-start | bytes 294920 | tf_op jit(solution)/shard_map/ppermute | solution.py:400
  359.5 10.8 %collective-permute-start.8 = (f32[1,64,384]{2,1,0:T(8,128)}, f32[1,64,384]{2,1,0:T(8,128)S(1)}, u32[]{:S(2)}, u32[]{:S(2)}) collective-permute-start(f32[1,64,384]{2,1,0:T(8,128)} %get-tuple-element.42), channel_id=1, source_target_pairs={{0,2},{1,3},{2,0},{3,1},{16,18},{17,19},{18,16},{19,17},{4,6},{5,7... | collective-permute-start | bytes 294920 | tf_op jit(solution)/shard_map/ppermute | solution.py:400
  362.8 7.4 %collective-permute-start.7 = (f32[1,64,384]{2,1,0:T(8,128)S(1)}, f32[1,64,384]{2,1,0:T(8,128)S(1)}, u32[]{:S(2)}, u32[]{:S(2)}) collective-permute-start(f32[1,64,384]{2,1,0:T(8,128)S(1)} %get-tuple-element.43), channel_id=1, source_target_pairs={{0,1},{1,0},{2,3},{3,2},{16,17},{17,16},{18,19},{19,18},{4,5},{5,4... | collective-permute-start | bytes 294920 | tf_op jit(solution)/shard_map/ppermute | solution.py:400
  370.3 14.8 %copy-start.3 = (f32[8,8,8,768]{3,2,1,0:T(8,128)S(1)}, f32[8,8,8,768]{3,2,1,0:T(8,128)}, u32[]{:S(2)}) copy-start(f32[8,8,8,768]{3,2,1,0:T(8,128)} %copy-done.2) | copy-start | bytes 4718596
  393.8 0.8 copy-start.13
  394.6 0.8 copy-start.15
  395.4 5.0 copy-start.4
  395.4 5.0 copy-start.14
  395.4 5.0 copy-start.16
  395.4 144.0 %all-to-all-start.5 = ((f32[8,8,64,384]{3,2,1,0:T(8,128)}), f32[8,8,64,384]{3,2,1,0:T(8,128)}, u32[]{:S(2)}, u32[]{:S(2)}) async-start(f32[8,8,64,384]{3,2,1,0:T(8,128)} %shard_map.80), calls=%async_computation.5 | async-start | bytes 12582912 | tf_op jit(solution)/shard_map/all_to_all | solution.py:390
  539.3 149.2 %all-to-all-start.3 = ((f32[8,8,64,128]{3,2,1,0:T(8,128)}), f32[8,8,64,128]{3,2,1,0:T(8,128)}, u32[]{:S(2)}, u32[]{:S(2)}) async-start(f32[8,8,64,128]{3,2,1,0:T(8,128)} %shard_map.78), calls=%async_computation.3 | async-start | bytes 4194304 | tf_op jit(solution)/shard_map/all_to_all | solution.py:390
  548.9 6.4 copy-start.1
  550.8 38.8 %collective-permute-start.20 = (f32[1,8,64,128]{3,2,1,0:T(8,128)S(1)}, f32[1,8,64,128]{3,2,1,0:T(8,128)S(1)}, u32[]{:S(2)}, u32[]{:S(2)}) collective-permute-start(f32[1,8,64,128]{3,2,1,0:T(8,128)S(1)} %get-tuple-element.29), channel_id=1, source_target_pairs={{0,19},{1,18},{2,17},{3,16},{16,3},{17,2},{18,1},{19,0},{4,23},{5,... | collective-permute-start | bytes 786440 | tf_op jit(solution)/shard_map/ppermute | solution.py:400
  555.2 74.0 %collective-permute-start.19 = (f32[1,8,64,128]{3,2,1,0:T(8,128)S(1)}, f32[1,8,64,128]{3,2,1,0:T(8,128)S(1)}, u32[]{:S(2)}, u32[]{:S(2)}) collective-permute-start(f32[1,8,64,128]{3,2,1,0:T(8,128)S(1)} %get-tuple-element.30), channel_id=1, source_target_pairs={{0,18},{1,19},{2,16},{3,17},{16,2},{17,3},{18,0},{19,1},{4,22},{5,... | collective-permute-start | bytes 786440 | tf_op jit(solution)/shard_map/ppermute | solution.py:400
  561.8 70.4 %collective-permute-start.27 = (f32[1,8,64,128]{3,2,1,0:T(8,128)S(1)}, f32[1,8,64,128]{3,2,1,0:T(8,128)S(1)}, u32[]{:S(2)}, u32[]{:S(2)}) collective-permute-start(f32[1,8,64,128]{3,2,1,0:T(8,128)S(1)} %get-tuple-element.21), channel_id=1, source_target_pairs={{0,19},{1,18},{2,17},{3,16},{16,3},{17,2},{18,1},{19,0},{4,23},{5,... | collective-permute-start | bytes 786440 | tf_op jit(solution)/shard_map/ppermute | solution.py:400
  564.7 86.9 %collective-permute-start.26 = (f32[1,8,64,128]{3,2,1,0:T(8,128)S(1)}, f32[1,8,64,128]{3,2,1,0:T(8,128)S(1)}, u32[]{:S(2)}, u32[]{:S(2)}) collective-permute-start(f32[1,8,64,128]{3,2,1,0:T(8,128)S(1)} %get-tuple-element.22), channel_id=1, source_target_pairs={{0,18},{1,19},{2,16},{3,17},{16,2},{17,3},{18,0},{19,1},{4,22},{5,... | collective-permute-start | bytes 786440 | tf_op jit(solution)/shard_map/ppermute | solution.py:400
  565.7 85.9 %collective-permute-start.25 = (f32[1,8,64,128]{3,2,1,0:T(8,128)S(1)}, f32[1,8,64,128]{3,2,1,0:T(8,128)S(1)}, u32[]{:S(2)}, u32[]{:S(2)}) collective-permute-start(f32[1,8,64,128]{3,2,1,0:T(8,128)S(1)} %get-tuple-element.23), channel_id=1, source_target_pairs={{0,17},{1,16},{2,19},{3,18},{16,1},{17,0},{18,3},{19,2},{4,21},{5,... | collective-permute-start | bytes 786440 | tf_op jit(solution)/shard_map/ppermute | solution.py:400
  589.5 63.8 %collective-permute-start.24 = (f32[1,8,64,128]{3,2,1,0:T(8,128)S(1)}, f32[1,8,64,128]{3,2,1,0:T(8,128)S(1)}, u32[]{:S(2)}, u32[]{:S(2)}) collective-permute-start(f32[1,8,64,128]{3,2,1,0:T(8,128)S(1)} %get-tuple-element.24), channel_id=1, source_target_pairs={{0,16},{1,17},{2,18},{3,19},{16,0},{17,1},{18,2},{19,3},{4,20},{5,... | collective-permute-start | bytes 786440 | tf_op jit(solution)/shard_map/ppermute | solution.py:400
  629.2 26.0 %collective-permute-start.23 = (f32[1,8,64,128]{3,2,1,0:T(8,128)S(1)}, f32[1,8,64,128]{3,2,1,0:T(8,128)S(1)}, u32[]{:S(2)}, u32[]{:S(2)}) collective-permute-start(f32[1,8,64,128]{3,2,1,0:T(8,128)S(1)} %get-tuple-element.25), channel_id=1, source_target_pairs={{0,3},{1,2},{2,1},{3,0},{16,19},{17,18},{18,17},{19,16},{4,7},{5,6... | collective-permute-start | bytes 786440 | tf_op jit(solution)/shard_map/ppermute | solution.py:400
  632.2 27.1 %collective-permute-start.22 = (f32[1,8,64,128]{3,2,1,0:T(8,128)S(1)}, f32[1,8,64,128]{3,2,1,0:T(8,128)S(1)}, u32[]{:S(2)}, u32[]{:S(2)}) collective-permute-start(f32[1,8,64,128]{3,2,1,0:T(8,128)S(1)} %get-tuple-element.26), channel_id=1, source_target_pairs={{0,2},{1,3},{2,0},{3,1},{16,18},{17,19},{18,16},{19,17},{4,6},{5,7... | collective-permute-start | bytes 786440 | tf_op jit(solution)/shard_map/ppermute | solution.py:400
  651.6 13.1 %collective-permute-start.21 = (f32[1,8,64,128]{3,2,1,0:T(8,128)S(1)}, f32[1,8,64,128]{3,2,1,0:T(8,128)S(1)}, u32[]{:S(2)}, u32[]{:S(2)}) collective-permute-start(f32[1,8,64,128]{3,2,1,0:T(8,128)S(1)} %get-tuple-element.27), channel_id=1, source_target_pairs={{0,1},{1,0},{2,3},{3,2},{16,17},{17,16},{18,19},{19,18},{4,5},{5,4... | collective-permute-start | bytes 786440 | tf_op jit(solution)/shard_map/ppermute | solution.py:400
  651.7 25.6 %collective-permute-start.18 = (f32[1,8,64,128]{3,2,1,0:T(8,128)S(1)}, f32[1,8,64,128]{3,2,1,0:T(8,128)S(1)}, u32[]{:S(2)}, u32[]{:S(2)}) collective-permute-start(f32[1,8,64,128]{3,2,1,0:T(8,128)S(1)} %get-tuple-element.31), channel_id=1, source_target_pairs={{0,17},{1,16},{2,19},{3,18},{16,1},{17,0},{18,3},{19,2},{4,21},{5,... | collective-permute-start | bytes 786440 | tf_op jit(solution)/shard_map/ppermute | solution.py:400
  653.3 23.9 %collective-permute-start.17 = (f32[1,8,64,128]{3,2,1,0:T(8,128)S(1)}, f32[1,8,64,128]{3,2,1,0:T(8,128)S(1)}, u32[]{:S(2)}, u32[]{:S(2)}) collective-permute-start(f32[1,8,64,128]{3,2,1,0:T(8,128)S(1)} %get-tuple-element.32), channel_id=1, source_target_pairs={{0,16},{1,17},{2,18},{3,19},{16,0},{17,1},{18,2},{19,3},{4,20},{5,... | collective-permute-start | bytes 786440 | tf_op jit(solution)/shard_map/ppermute | solution.py:400
  655.1 22.1 %collective-permute-start.16 = (f32[1,8,64,128]{3,2,1,0:T(8,128)S(1)}, f32[1,8,64,128]{3,2,1,0:T(8,128)S(1)}, u32[]{:S(2)}, u32[]{:S(2)}) collective-permute-start(f32[1,8,64,128]{3,2,1,0:T(8,128)S(1)} %get-tuple-element.33), channel_id=1, source_target_pairs={{0,3},{1,2},{2,1},{3,0},{16,19},{17,18},{18,17},{19,16},{4,7},{5,6... | collective-permute-start | bytes 786440 | tf_op jit(solution)/shard_map/ppermute | solution.py:400
  659.3 22.6 %collective-permute-start.15 = (f32[1,8,64,128]{3,2,1,0:T(8,128)S(1)}, f32[1,8,64,128]{3,2,1,0:T(8,128)S(1)}, u32[]{:S(2)}, u32[]{:S(2)}) collective-permute-start(f32[1,8,64,128]{3,2,1,0:T(8,128)S(1)} %get-tuple-element.34), channel_id=1, source_target_pairs={{0,2},{1,3},{2,0},{3,1},{16,18},{17,19},{18,16},{19,17},{4,6},{5,7... | collective-permute-start | bytes 786440 | tf_op jit(solution)/shard_map/ppermute | solution.py:400
  664.8 20.4 %collective-permute-start.14 = (f32[1,8,64,128]{3,2,1,0:T(8,128)S(1)}, f32[1,8,64,128]{3,2,1,0:T(8,128)S(1)}, u32[]{:S(2)}, u32[]{:S(2)}) collective-permute-start(f32[1,8,64,128]{3,2,1,0:T(8,128)S(1)} %get-tuple-element.35), channel_id=1, source_target_pairs={{0,1},{1,0},{2,3},{3,2},{16,17},{17,16},{18,19},{19,18},{4,5},{5,4... | collective-permute-start | bytes 786440 | tf_op jit(solution)/shard_map/ppermute | solution.py:400

commit v4 on v3

--- a/solution.py
+++ b/solution.py
@@ -36,9 +36,19 @@
 
 
 def forecast_body(x_ref, low_ref, high_ref, coeff_ref, *refs):
-    outs, (even_ref, odd_ref) = refs[:-2], refs[-2:]
-    _, rows, lon = x_ref.shape
+    outs, (even_ref, odd_ref, wide_ref) = refs[:-3], refs[-3:]
+    group, rows, lon = x_ref.shape
     halo = FSTEPS
+
+    @pl.when(pl.program_id(0) == 0)
+    def _():
+        def widen(row, carry):
+            for k in range(5):
+                wide_ref[k, row] = jnp.broadcast_to(coeff_ref[k, pl.ds(row, 1), :], (8, lon))
+            return carry
+
+        lax.fori_loop(0, rows + 2 * halo, widen, 0, unroll=4)
+
     even_ref[0:halo] = jnp.swapaxes(low_ref[...], 0, 1)
     even_ref[halo + rows : 2 * halo + rows] = jnp.swapaxes(high_ref[...], 0, 1)
     for first in range(0, rows, 8):
@@ -53,7 +63,7 @@
                 here = src[row]
                 east = pltpu.roll(here, lon - 1, 1)
                 west = pltpu.roll(here, 1, 1)
-                c = [coeff_ref[k, pl.ds(row, 1), :] for k in range(5)]
+                c = [jnp.concatenate([wide_ref[k, row]] * (group // 8)) for k in range(5)]
                 dst[row] = (
                     c[0] * here + c[1] * west + c[2] * east + c[3] * src[row - 1] + c[4] * src[row + 1]
                 )
@@ -93,7 +103,8 @@
         ],
         out_specs=[pl.BlockSpec((rows, group, lanes), lambda i: (0, i, 0)) for lanes in widths],
         out_shape=[pltpu.HBM((rows, count, lanes), F32) for lanes in widths],
-        scratch_shapes=[pltpu.VMEM((total, group, lon), F32)] * 2,
+        scratch_shapes=[pltpu.VMEM((total, group, lon), F32)] * 2
+        + [pltpu.VMEM((5, total, 8, lon), F32)],
     )(x, low, high, coeffs)
 
 
@@ -443,7 +454,7 @@
         state = forecast(starting_states, *halos, coeffs, start, at, count, parts)
         at += count
         states.append(state)
-        if i == 0 and len(layout) > 2:
+        if i == 1 and len(layout) > 2:
             later, _ = lax.optimization_barrier((starting_states, state[0]))
             halos_rest = edges(later[layout[2][0] : layout[2][0] + layout[2][1]])
     received = []

time: 697 us -> 693 us (level)
  Pallas kernels: 177 us -> 170 us
    pallas_call x3, Pallas kernels: 109 us -> 102 us  [forecast(): call(forecast_body, flops=9 * FSTEPS * total * count * lon, moved=8 * cou...]
  transfers between devices with their start and end apart: 33 -> 33, of which waited for: 19 -> 20; matrix products, arithmetic and copies ran while one was open for 1% -> 1% of each run, Pallas kernels for 22% -> 22%
where the time goes in v4:
time: 693 us; the launch traced here: 691 us
  waiting for transfers between devices  293 us (42%)
  Pallas kernels  170 us (25%)
  blocking collectives  119 us (17%)
  starting transfers between devices  91.1 us (13%)
  local copies, waits for them, and re-layouts  16.7 us (2%)
    all_to_all x5, waiting for transfers between devices, exchange(): return lax.all_to_all(array, GROUP, split_axis=0, concat_axis=0, tiled=True)  142 us
    all_to_all x1, blocking collectives, exchange(): return lax.all_to_all(array, GROUP, split_axis=0, concat_axis=0, tiled=True)  119 us
    pallas_call x3, Pallas kernels, forecast(): call(forecast_body, flops=9 * FSTEPS * total * count * lon, moved=8 * cou...  102 us
    ppermute x21, waiting for transfers between devices, exchange_by_steps(): lax.ppermute(piece, GROUP, [(i, i ^ step) for i in range(size)])  92.2 us
    ppermute x3, waiting for transfers between devices, gathered(): other = lax.ppermute(row, GROUP, [(i, i ^ bit) for i in range(size)])  54.9 us
    ppermute x21, starting transfers between devices, exchange_by_steps(): lax.ppermute(piece, GROUP, [(i, i ^ step) for i in range(size)])  45.9 us
    all_to_all x5, starting transfers between devices, exchange(): return lax.all_to_all(array, GROUP, split_axis=0, concat_axis=0, tiled=True)  28.1 us
    pallas_call x4, Pallas kernels, analyse(): call(functools.partial(analyse_body, layout), flops=6 * size * size * blo...  23.4 us
  transfers between devices with their start and end apart: 33, of which 20 were waited for; matrix products, arithmetic and copies ran while one was open for 1% of the time, Pallas kernels for 22%

profile of v4, /device:TPU:0, one launch (start us, length us, event | category | flops | bytes accessed | tf_op | source)
XLA Modules:
  0.0 691.3 jit_solution(11193188468178855939)
XLA Ops:
  0.0 1.1 fusion.6
  1.1 1.2 fusion.7
  2.4 1.3 collective-permute-start.4
  3.7 3.1 collective-permute-start.3
  6.9 1.6 collective-permute-done.3
  9.0 15.7 %shard_map.73.refs_0_ = f32[64,8,768]{2,1,0:T(8,128)} custom-call(f32[64,64,768]{2,1,0:T(8,128)} %x_ref.5, f32[24,8,768]{2,1,0:T(8,128)S(1)} %slice.80.low_ref, f32[24,8,768]{2,1,0:T(8,128)S(1)} %slice.81.high_ref, f32[5,104,768]{2,1,0:T(8,128)S(1)} %subtract_dynamic-update-slice_fusion.coeff_ref), custom_call_target="tpu_custom_call" | custom-call | flops 46006272 | bytes 3145728 | tf_op jit(solution)/shard_map/pallas_call | solution.py:93
  24.7 7.3 %all-to-all-start = ((f32[8,8,8,768]{3,2,1,0:T(8,128)}), f32[8,8,8,768]{3,2,1,0:T(8,128)S(1)}, u32[]{:S(2)}, u32[]{:S(2)}) async-start(f32[8,8,8,768]{3,2,1,0:T(8,128)} %bitcast.23), calls=%async_computation | async-start | bytes 3145728 | tf_op jit(solution)/shard_map/all_to_all | solution.py:401
  33.1 1.1 copy-done.12
  34.2 26.2 %shard_map.74.refs_1_ = f32[64,16,768]{2,1,0:T(8,128)} custom-call(f32[64,64,768]{2,1,0:T(8,128)} %x_ref.5, f32[24,8,768]{2,1,0:T(8,128)S(1)} %copy-done.12, f32[24,8,768]{2,1,0:T(8,128)S(1)} %copy-done.10, f32[5,104,768]{2,1,0:T(8,128)S(1)} %subtract_dynamic-update-slice_fusion.coeff_ref), custom_call_target="tpu_custom_call" | custom-call | flops 92012544 | bytes 6291456 | tf_op jit(solution)/shard_map/pallas_call | solution.py:93
  60.4 6.0 all-to-all-done.refs_0_
  66.4 1.2 copy-done.2
  67.5 6.6 all-to-all-start.1
  74.1 1.8 fusion.5
  75.9 1.3 collective-permute-start.6
  77.2 4.7 collective-permute-start.5
  81.9 2.1 collective-permute-done.5.low_ref
  84.0 60.1 %shard_map.75 = (f32[64,40,512]{2,1,0:T(8,128)}, f32[64,40,256]{2,1,0:T(8,128)}) custom-call(f32[64,64,768]{2,1,0:T(8,128)} %x_ref.5, f32[40,8,768]{2,1,0:T(8,128)S(1)} %collective-permute-done.5.low_ref, f32[40,8,768]{2,1,0:T(8,128)S(1)} %collective-permute-done.6.high_ref, f32[5,104,768]{2,1,0:T(8,128)S(1)} %copy-done.6), custom_call_target="tpu_custom_call" | custom-call | flops 230031360 | bytes 15728640 | tf_op jit(solution)/shard_map/pallas_call | solution.py:93
  144.1 2.0 all-to-all-done.1.refs_1_
  146.1 119.0 %all_to_all.30.refs_2_ = f32[8,8,40,512]{3,2,1,0:T(8,128)} all-to-all(f32[8,8,40,512]{3,2,1,0:T(8,128)} %bitcast.28), channel_id=1, replica_groups=mesh['members'=2,'lat'=4,'blk'=4] {'members','blk'}, dimensions={0} | all-to-all | bytes 10485760 | tf_op jit(solution)/shard_map/all_to_all | solution.py:401
  265.0 4.7 all-to-all-start.2
  269.8 1.8 collective-permute-start
  271.6 40.1 %collective-permute-done = f32[1,2,128]{2,1,0:T(2,128)S(1)} collective-permute-done((f32[1,2,128]{2,1,0:T(2,128)S(1)}, f32[1,2,128]{2,1,0:T(2,128)S(1)}, u32[]{:S(2)}, u32[]{:S(2)}) %collective-permute-start) | collective-permute-done | bytes 1056 | tf_op jit(solution)/shard_map/ppermute | solution.py:392
  311.7 3.7 collective-permute-start.1
  315.4 12.5 %collective-permute-done.1 = f32[2,2,128]{2,1,0:T(2,128)S(1)} collective-permute-done((f32[2,2,128]{2,1,0:T(2,128)S(1)}, f32[2,2,128]{2,1,0:T(2,128)S(1)}, u32[]{:S(2)}, u32[]{:S(2)}) %collective-permute-start.1) | collective-permute-done | bytes 2080 | tf_op jit(solution)/shard_map/ppermute | solution.py:392
  327.9 1.3 collective-permute-start.2
  329.1 2.3 collective-permute-done.2
  331.5 1.4 copy-done.7
  332.9 1.7 copy-done.8
  334.6 9.5 %shard_map.76 = f32[8,64,128]{2,1,0:T(8,128)S(1)} custom-call(s32[8,1,128]{2,1,0:T(1,128)S(1)} %get-tuple-element.50.cells_ref, f32[64,8,768]{2,1,0:T(8,128)S(1)} %copy-done.7, f32[64,16,768]{2,1,0:T(8,128)} %shard_map.74.refs_1_, f32[64,40,512]{2,1,0:T(8,128)} %get-tuple-element.11.refs_2_, f32[64,40,256]{2,1,0:T(8,128)S(1)} %copy-done.8), custom_call_target="tpu_custom_call" | custom-call | flops 2415919104 | bytes 12582912 | tf_op jit(solution)/shard_map/pallas_call | solution.py:145
  345.1 4.9 collective-permute-start.13
  350.0 1.1 collective-permute-start.11
  352.0 3.5 collective-permute-start.9
  355.5 3.3 collective-permute-done.12.refs_6_
  358.8 1.4 collective-permute-done.10.refs_4_
  361.0 5.6 collective-permute-done.8.refs_2_
  366.6 14.8 %shard_map.77 = (bf16[512,512]{1,0:T(8,128)(2,1)S(1)}, bf16[512,512]{1,0:T(8,128)(2,1)S(1)}) custom-call(s32[1]{0:T(128)} %bitcast.me_ref, f32[1,64,384]{2,1,0:T(8,128)S(1)} %get-tuple-element.44.refs_0_, f32[1,64,384]{2,1,0:T(8,128)S(1)} %collective-permute-done.7.refs_1_, f32[1,64,384]{2,1,0:T(8,128)S(1)} %collective-permute-done.8.refs_2_, ...), custom_call_target="tpu_custom_call" | custom-call | flops 16106127360 | bytes 1835008 | tf_op jit(solution)/shard_map/pallas_call | solution.py:249
  381.4 8.7 %shard_map.80 = f32[8,8,64,384]{3,2,1,0:T(8,128)} custom-call(bf16[512,512]{1,0:T(8,128)(2,1)S(1)} %get-tuple-element.13.mix_top_ref, bf16[512,512]{1,0:T(8,128)(2,1)S(1)} %get-tuple-element.14.mix_low_ref, f32[8,8,8,768]{3,2,1,0:T(8,128)S(1)} %copy-done.3, f32[8,8,16,768]{3,2,1,0:T(8,128)S(1)} %all-to-all-done.1.refs_1_, f32[8,8,40,512]{3,2,1,0:T(8,128)} %all_to_all.30.refs_2_), custom_call_target="tpu_custom_call" | custom-call | flops 4831838208 | bytes 12582912 | tf_op jit(solution)/shard_map/pallas_call | solution.py:301
  391.6 4.9 all-to-all-start.5
  396.6 5.0 shard_map.78
  401.6 134.5 %all-to-all-done.5 = f32[8,8,64,384]{3,2,1,0:T(8,128)} async-done(((f32[8,8,64,384]{3,2,1,0:T(8,128)}), f32[8,8,64,384]{3,2,1,0:T(8,128)}, u32[]{:S(2)}, u32[]{:S(2)}) %all-to-all-start.5) | async-done | bytes 6291488 | tf_op jit(solution)/shard_map/all_to_all | solution.py:401
  536.1 4.6 all-to-all-start.3
  540.7 5.0 shard_map.79
  545.6 1.9 constant_dynamic-slice_fusion.8
  547.5 4.5 collective-permute-start.20
  552.0 4.8 shard_map.81
  556.8 1.7 constant_dynamic-slice_fusion
  558.5 3.0 collective-permute-start.27
  562.5 1.9 collective-permute-start.25
  564.4 22.0 %collective-permute-done.20.refs_7_ = f32[1,8,64,128]{3,2,1,0:T(8,128)S(1)} collective-permute-done((f32[1,8,64,128]{3,2,1,0:T(8,128)S(1)}, f32[1,8,64,128]{3,2,1,0:T(8,128)S(1)}, u32[]{:S(2)}, u32[]{:S(2)}) %collective-permute-start.20) | collective-permute-done | bytes 262176 | tf_op jit(solution)/shard_map/ppermute | solution.py:411
  586.9 37.7 %collective-permute-done.19.refs_6_ = f32[1,8,64,128]{3,2,1,0:T(8,128)S(1)} collective-permute-done((f32[1,8,64,128]{3,2,1,0:T(8,128)S(1)}, f32[1,8,64,128]{3,2,1,0:T(8,128)S(1)}, u32[]{:S(2)}, u32[]{:S(2)}) %collective-permute-start.19) | collective-permute-done | bytes 262176 | tf_op jit(solution)/shard_map/ppermute | solution.py:411
  624.6 4.5 collective-permute-start.23
  629.1 10.4 %collective-permute-start.22 = (f32[1,8,64,128]{3,2,1,0:T(8,128)S(1)}, f32[1,8,64,128]{3,2,1,0:T(8,128)S(1)}, u32[]{:S(2)}, u32[]{:S(2)}) collective-permute-start(f32[1,8,64,128]{3,2,1,0:T(8,128)S(1)} %get-tuple-element.26), channel_id=1, source_target_pairs={{0,2},{1,3},{2,0},{3,1},{16,18},{17,19},{18,16},{19,17},{4,6},{5,7... | collective-permute-start | bytes 786440 | tf_op jit(solution)/shard_map/ppermute | solution.py:411
  639.4 7.7 %collective-permute-done.26.refs_6_ = f32[1,8,64,128]{3,2,1,0:T(8,128)S(1)} collective-permute-done((f32[1,8,64,128]{3,2,1,0:T(8,128)S(1)}, f32[1,8,64,128]{3,2,1,0:T(8,128)S(1)}, u32[]{:S(2)}, u32[]{:S(2)}) %collective-permute-start.26) | collective-permute-done | bytes 262176 | tf_op jit(solution)/shard_map/ppermute | solution.py:411
  647.8 1.3 collective-permute-start.18
  649.1 1.5 collective-permute-start.17
  650.6 4.5 collective-permute-start.16
  655.8 4.9 collective-permute-done.21.refs_1_
  660.7 1.8 collective-permute-start.14
  662.5 3.3 shard_map.82.refs_0_
  665.8 8.0 %shard_map.83.refs_8_ = f32[64,64,768]{2,1,0:T(8,128)} custom-call(f32[64,64,384]{2,1,0:T(8,128)} %bitcast.14.part_ref, f32[64,64,768]{2,1,0:T(8,128)} %shard_map.82.refs_0_), custom_call_target="tpu_custom_call", output_to_operand_aliasing={{}: (1, {})} | custom-call | bytes 12582912 | tf_op jit(solution)/shard_map/pallas_call | solution.py:324
  673.9 4.9 collective-permute-done.15.refs_2_
  678.8 3.4 collective-permute-done.14.refs_1_
  682.2 3.3 shard_map.84.refs_0_
  685.5 5.7 shard_map.85
  (92 shorter events, 9.0 us)
Async XLA Ops:
  0.0 2.3 copy-start.18
  0.0 2.3 copy-start.19
  0.0 2.3 copy-start.20
  2.4 4.5 collective-permute-start.4
  3.7 4.8 collective-permute-start.3
  8.8 23.2 %copy-start.5 = (f32[5,104,768]{2,1,0:T(8,128)}, f32[5,104,768]{2,1,0:T(8,128)S(1)}, u32[]{:S(2)}) copy-start(f32[5,104,768]{2,1,0:T(8,128)S(1)} %subtract_dynamic-update-slice_fusion.coeff_ref) | copy-start | bytes 4792324
  8.9 15.8 %copy-start.9 = (f32[24,8,768]{2,1,0:T(8,128)}, f32[24,8,768]{2,1,0:T(8,128)S(1)}, u32[]{:S(2)}) copy-start(f32[24,8,768]{2,1,0:T(8,128)S(1)} %slice.81.high_ref) | copy-start | bytes 1769476
  9.0 15.7 %copy-start.11 = (f32[24,8,768]{2,1,0:T(8,128)}, f32[24,8,768]{2,1,0:T(8,128)S(1)}, u32[]{:S(2)}) copy-start(f32[24,8,768]{2,1,0:T(8,128)S(1)} %slice.80.low_ref) | copy-start | bytes 1769476
  24.7 41.7 %all-to-all-start = ((f32[8,8,8,768]{3,2,1,0:T(8,128)}), f32[8,8,8,768]{3,2,1,0:T(8,128)S(1)}, u32[]{:S(2)}, u32[]{:S(2)}) async-start(f32[8,8,8,768]{3,2,1,0:T(8,128)} %bitcast.23), calls=%async_computation | async-start | bytes 3145728 | tf_op jit(solution)/shard_map/all_to_all | solution.py:401
  32.0 1.1 copy-start.10
  33.1 1.1 copy-start.12
  66.4 1.2 copy-start.2
  67.5 78.5 %all-to-all-start.1 = ((f32[8,8,16,768]{3,2,1,0:T(8,128)}), f32[8,8,16,768]{3,2,1,0:T(8,128)S(1)}, u32[]{:S(2)}, u32[]{:S(2)}) async-start(f32[8,8,16,768]{3,2,1,0:T(8,128)} %bitcast.27), calls=%async_computation.1 | async-start | bytes 6291456 | tf_op jit(solution)/shard_map/all_to_all | solution.py:401
  74.1 9.9 %copy-start.6 = (f32[5,104,768]{2,1,0:T(8,128)S(1)}, f32[5,104,768]{2,1,0:T(8,128)}, u32[]{:S(2)}) copy-start(f32[5,104,768]{2,1,0:T(8,128)} %copy-done.5) | copy-start | bytes 4792324
  75.9 6.0 collective-permute-start.6
  77.2 6.8 collective-permute-start.5
  146.1 235.3 %copy-start = (f32[8,8,16,768]{3,2,1,0:T(8,128)}, f32[8,8,16,768]{3,2,1,0:T(8,128)S(1)}, u32[]{:S(2)}) copy-start(f32[8,8,16,768]{3,2,1,0:T(8,128)S(1)} %all-to-all-done.1.refs_1_) | copy-start | bytes 9437188
  265.0 4.7 copy-start.22
  265.0 4.7 copy-start.21
  265.0 126.6 %all-to-all-start.2 = ((f32[8,8,40,256]{3,2,1,0:T(8,128)}), f32[8,8,40,256]{3,2,1,0:T(8,128)}, u32[]{:S(2)}, u32[]{:S(2)}) async-start(f32[8,8,40,256]{3,2,1,0:T(8,128)} %bitcast.24), calls=%async_computation.2 | async-start | bytes 5242880 | tf_op jit(solution)/shard_map/all_to_all | solution.py:401
  269.8 41.9 %collective-permute-start = (f32[1,2,128]{2,1,0:T(2,128)S(1)}, f32[1,2,128]{2,1,0:T(2,128)S(1)}, u32[]{:S(2)}, u32[]{:S(2)}) collective-permute-start(f32[1,2,128]{2,1,0:T(2,128)S(1)} %maximum_bitcast_fusion), channel_id=1, source_target_pairs={{0,1},{1,0},{2,3},{3,2},{16,17},{17,16},{18,19},{19,18},{4,5},{5,4... | collective-permute-start | bytes 3080 | tf_op jit(solution)/shard_map/ppermute | solution.py:392
  311.7 16.2 %collective-permute-start.1 = (f32[2,2,128]{2,1,0:T(2,128)S(1)}, f32[2,2,128]{2,1,0:T(2,128)S(1)}, u32[]{:S(2)}, u32[]{:S(2)}) collective-permute-start(f32[2,2,128]{2,1,0:T(2,128)S(1)} %maximum_select_fusion.2), channel_id=1, source_target_pairs={{0,2},{1,3},{2,0},{3,1},{16,18},{17,19},{18,16},{19,17},{4,6},{5,7... | collective-permute-start | bytes 6152 | tf_op jit(solution)/shard_map/ppermute | solution.py:392
  327.9 3.6 collective-permute-start.2
  331.5 1.4 copy-start.7
  332.9 1.7 copy-start.8
  344.2 22.4 %copy-start.17 = (f32[1,1,3,128]{3,1,2,0:T(1,128)S(1)}, f32[1,1,3,128]{3,1,2,0:T(1,128)}, u32[]{:S(2)}) copy-start(f32[1,1,3,128]{3,1,2,0:T(1,128)} %param.13) | copy-start | bytes 4612
  345.1 10.4 %collective-permute-start.13 = (f32[1,64,384]{2,1,0:T(8,128)}, f32[1,64,384]{2,1,0:T(8,128)S(1)}, u32[]{:S(2)}, u32[]{:S(2)}) collective-permute-start(f32[1,64,384]{2,1,0:T(8,128)} %get-tuple-element.37), channel_id=1, source_target_pairs={{0,19},{1,18},{2,17},{3,16},{16,3},{17,2},{18,1},{19,0},{4,23},{5,... | collective-permute-start | bytes 294920 | tf_op jit(solution)/shard_map/ppermute | solution.py:411
  350.0 8.8 %collective-permute-start.12 = (f32[1,64,384]{2,1,0:T(8,128)}, f32[1,64,384]{2,1,0:T(8,128)S(1)}, u32[]{:S(2)}, u32[]{:S(2)}) collective-permute-start(f32[1,64,384]{2,1,0:T(8,128)} %get-tuple-element.38), channel_id=1, source_target_pairs={{0,18},{1,19},{2,16},{3,17},{16,2},{17,3},{18,0},{19,1},{4,22},{5,... | collective-permute-start | bytes 294920 | tf_op jit(solution)/shard_map/ppermute | solution.py:411
  350.0 8.8 %collective-permute-start.11 = (f32[1,64,384]{2,1,0:T(8,128)}, f32[1,64,384]{2,1,0:T(8,128)S(1)}, u32[]{:S(2)}, u32[]{:S(2)}) collective-permute-start(f32[1,64,384]{2,1,0:T(8,128)} %get-tuple-element.39), channel_id=1, source_target_pairs={{0,17},{1,16},{2,19},{3,18},{16,1},{17,0},{18,3},{19,2},{4,21},{5,... | collective-permute-start | bytes 294920 | tf_op jit(solution)/shard_map/ppermute | solution.py:411
  351.1 9.1 %collective-permute-start.10 = (f32[1,64,384]{2,1,0:T(8,128)}, f32[1,64,384]{2,1,0:T(8,128)S(1)}, u32[]{:S(2)}, u32[]{:S(2)}) collective-permute-start(f32[1,64,384]{2,1,0:T(8,128)} %get-tuple-element.40), channel_id=1, source_target_pairs={{0,16},{1,17},{2,18},{3,19},{16,0},{17,1},{18,2},{19,3},{4,20},{5,... | collective-permute-start | bytes 294920 | tf_op jit(solution)/shard_map/ppermute | solution.py:411
  352.0 9.0 %collective-permute-start.9 = (f32[1,64,384]{2,1,0:T(8,128)}, f32[1,64,384]{2,1,0:T(8,128)S(1)}, u32[]{:S(2)}, u32[]{:S(2)}) collective-permute-start(f32[1,64,384]{2,1,0:T(8,128)} %get-tuple-element.41), channel_id=1, source_target_pairs={{0,3},{1,2},{2,1},{3,0},{16,19},{17,18},{18,17},{19,16},{4,7},{5,6... | collective-permute-start | bytes 294920 | tf_op jit(solution)/shard_map/ppermute | solution.py:411
  355.5 11.0 %collective-permute-start.8 = (f32[1,64,384]{2,1,0:T(8,128)}, f32[1,64,384]{2,1,0:T(8,128)S(1)}, u32[]{:S(2)}, u32[]{:S(2)}) collective-permute-start(f32[1,64,384]{2,1,0:T(8,128)} %get-tuple-element.42), channel_id=1, source_target_pairs={{0,2},{1,3},{2,0},{3,1},{16,18},{17,19},{18,16},{19,17},{4,6},{5,7... | collective-permute-start | bytes 294920 | tf_op jit(solution)/shard_map/ppermute | solution.py:411
  358.8 7.8 %collective-permute-start.7 = (f32[1,64,384]{2,1,0:T(8,128)S(1)}, f32[1,64,384]{2,1,0:T(8,128)S(1)}, u32[]{:S(2)}, u32[]{:S(2)}) collective-permute-start(f32[1,64,384]{2,1,0:T(8,128)S(1)} %get-tuple-element.43), channel_id=1, source_target_pairs={{0,1},{1,0},{2,3},{3,2},{16,17},{17,16},{18,19},{19,18},{4,5},{5,4... | collective-permute-start | bytes 294920 | tf_op jit(solution)/shard_map/ppermute | solution.py:411
  366.6 14.8 %copy-start.3 = (f32[8,8,8,768]{3,2,1,0:T(8,128)S(1)}, f32[8,8,8,768]{3,2,1,0:T(8,128)}, u32[]{:S(2)}) copy-start(f32[8,8,8,768]{3,2,1,0:T(8,128)} %copy-done.2) | copy-start | bytes 4718596
  390.1 0.8 copy-start.13
  390.8 0.8 copy-start.15
  391.6 5.0 copy-start.4
  391.6 5.0 copy-start.14
  391.6 5.0 copy-start.16
  391.6 144.5 %all-to-all-start.5 = ((f32[8,8,64,384]{3,2,1,0:T(8,128)}), f32[8,8,64,384]{3,2,1,0:T(8,128)}, u32[]{:S(2)}, u32[]{:S(2)}) async-start(f32[8,8,64,384]{3,2,1,0:T(8,128)} %shard_map.80), calls=%async_computation.5 | async-start | bytes 12582912 | tf_op jit(solution)/shard_map/all_to_all | solution.py:401
  536.1 149.4 %all-to-all-start.3 = ((f32[8,8,64,128]{3,2,1,0:T(8,128)}), f32[8,8,64,128]{3,2,1,0:T(8,128)}, u32[]{:S(2)}, u32[]{:S(2)}) async-start(f32[8,8,64,128]{3,2,1,0:T(8,128)} %shard_map.78), calls=%async_computation.3 | async-start | bytes 4194304 | tf_op jit(solution)/shard_map/all_to_all | solution.py:401
  545.6 6.4 copy-start.1
  547.5 38.9 %collective-permute-start.20 = (f32[1,8,64,128]{3,2,1,0:T(8,128)S(1)}, f32[1,8,64,128]{3,2,1,0:T(8,128)S(1)}, u32[]{:S(2)}, u32[]{:S(2)}) collective-permute-start(f32[1,8,64,128]{3,2,1,0:T(8,128)S(1)} %get-tuple-element.29), channel_id=1, source_target_pairs={{0,19},{1,18},{2,17},{3,16},{16,3},{17,2},{18,1},{19,0},{4,23},{5,... | collective-permute-start | bytes 786440 | tf_op jit(solution)/shard_map/ppermute | solution.py:411
  552.0 72.6 %collective-permute-start.19 = (f32[1,8,64,128]{3,2,1,0:T(8,128)S(1)}, f32[1,8,64,128]{3,2,1,0:T(8,128)S(1)}, u32[]{:S(2)}, u32[]{:S(2)}) collective-permute-start(f32[1,8,64,128]{3,2,1,0:T(8,128)S(1)} %get-tuple-element.30), channel_id=1, source_target_pairs={{0,18},{1,19},{2,16},{3,17},{16,2},{17,3},{18,0},{19,1},{4,22},{5,... | collective-permute-start | bytes 786440 | tf_op jit(solution)/shard_map/ppermute | solution.py:411
  558.5 70.5 %collective-permute-start.27 = (f32[1,8,64,128]{3,2,1,0:T(8,128)S(1)}, f32[1,8,64,128]{3,2,1,0:T(8,128)S(1)}, u32[]{:S(2)}, u32[]{:S(2)}) collective-permute-start(f32[1,8,64,128]{3,2,1,0:T(8,128)S(1)} %get-tuple-element.21), channel_id=1, source_target_pairs={{0,19},{1,18},{2,17},{3,16},{16,3},{17,2},{18,1},{19,0},{4,23},{5,... | collective-permute-start | bytes 786440 | tf_op jit(solution)/shard_map/ppermute | solution.py:411
  561.5 85.6 %collective-permute-start.26 = (f32[1,8,64,128]{3,2,1,0:T(8,128)S(1)}, f32[1,8,64,128]{3,2,1,0:T(8,128)S(1)}, u32[]{:S(2)}, u32[]{:S(2)}) collective-permute-start(f32[1,8,64,128]{3,2,1,0:T(8,128)S(1)} %get-tuple-element.22), channel_id=1, source_target_pairs={{0,18},{1,19},{2,16},{3,17},{16,2},{17,3},{18,0},{19,1},{4,22},{5,... | collective-permute-start | bytes 786440 | tf_op jit(solution)/shard_map/ppermute | solution.py:411
  562.5 85.4 %collective-permute-start.25 = (f32[1,8,64,128]{3,2,1,0:T(8,128)S(1)}, f32[1,8,64,128]{3,2,1,0:T(8,128)S(1)}, u32[]{:S(2)}, u32[]{:S(2)}) collective-permute-start(f32[1,8,64,128]{3,2,1,0:T(8,128)S(1)} %get-tuple-element.23), channel_id=1, source_target_pairs={{0,17},{1,16},{2,19},{3,18},{16,1},{17,0},{18,3},{19,2},{4,21},{5,... | collective-permute-start | bytes 786440 | tf_op jit(solution)/shard_map/ppermute | solution.py:411
  586.4 62.7 %collective-permute-start.24 = (f32[1,8,64,128]{3,2,1,0:T(8,128)S(1)}, f32[1,8,64,128]{3,2,1,0:T(8,128)S(1)}, u32[]{:S(2)}, u32[]{:S(2)}) collective-permute-start(f32[1,8,64,128]{3,2,1,0:T(8,128)S(1)} %get-tuple-element.24), channel_id=1, source_target_pairs={{0,16},{1,17},{2,18},{3,19},{16,0},{17,1},{18,2},{19,3},{4,20},{5,... | collective-permute-start | bytes 786440 | tf_op jit(solution)/shard_map/ppermute | solution.py:411
  624.6 26.0 %collective-permute-start.23 = (f32[1,8,64,128]{3,2,1,0:T(8,128)S(1)}, f32[1,8,64,128]{3,2,1,0:T(8,128)S(1)}, u32[]{:S(2)}, u32[]{:S(2)}) collective-permute-start(f32[1,8,64,128]{3,2,1,0:T(8,128)S(1)} %get-tuple-element.25), channel_id=1, source_target_pairs={{0,3},{1,2},{2,1},{3,0},{16,19},{17,18},{18,17},{19,16},{4,7},{5,6... | collective-permute-start | bytes 786440 | tf_op jit(solution)/shard_map/ppermute | solution.py:411
  629.1 26.7 %collective-permute-start.22 = (f32[1,8,64,128]{3,2,1,0:T(8,128)S(1)}, f32[1,8,64,128]{3,2,1,0:T(8,128)S(1)}, u32[]{:S(2)}, u32[]{:S(2)}) collective-permute-start(f32[1,8,64,128]{3,2,1,0:T(8,128)S(1)} %get-tuple-element.26), channel_id=1, source_target_pairs={{0,2},{1,3},{2,0},{3,1},{16,18},{17,19},{18,16},{19,17},{4,6},{5,7... | collective-permute-start | bytes 786440 | tf_op jit(solution)/shard_map/ppermute | solution.py:411
  647.1 13.6 %collective-permute-start.21 = (f32[1,8,64,128]{3,2,1,0:T(8,128)S(1)}, f32[1,8,64,128]{3,2,1,0:T(8,128)S(1)}, u32[]{:S(2)}, u32[]{:S(2)}) collective-permute-start(f32[1,8,64,128]{3,2,1,0:T(8,128)S(1)} %get-tuple-element.27), channel_id=1, source_target_pairs={{0,1},{1,0},{2,3},{3,2},{16,17},{17,16},{18,19},{19,18},{4,5},{5,4... | collective-permute-start | bytes 786440 | tf_op jit(solution)/shard_map/ppermute | solution.py:411
  647.8 26.1 %collective-permute-start.18 = (f32[1,8,64,128]{3,2,1,0:T(8,128)S(1)}, f32[1,8,64,128]{3,2,1,0:T(8,128)S(1)}, u32[]{:S(2)}, u32[]{:S(2)}) collective-permute-start(f32[1,8,64,128]{3,2,1,0:T(8,128)S(1)} %get-tuple-element.31), channel_id=1, source_target_pairs={{0,17},{1,16},{2,19},{3,18},{16,1},{17,0},{18,3},{19,2},{4,21},{5,... | collective-permute-start | bytes 786440 | tf_op jit(solution)/shard_map/ppermute | solution.py:411
  649.1 24.8 %collective-permute-start.17 = (f32[1,8,64,128]{3,2,1,0:T(8,128)S(1)}, f32[1,8,64,128]{3,2,1,0:T(8,128)S(1)}, u32[]{:S(2)}, u32[]{:S(2)}) collective-permute-start(f32[1,8,64,128]{3,2,1,0:T(8,128)S(1)} %get-tuple-element.32), channel_id=1, source_target_pairs={{0,16},{1,17},{2,18},{3,19},{16,0},{17,1},{18,2},{19,3},{4,20},{5,... | collective-permute-start | bytes 786440 | tf_op jit(solution)/shard_map/ppermute | solution.py:411
  650.6 23.3 %collective-permute-start.16 = (f32[1,8,64,128]{3,2,1,0:T(8,128)S(1)}, f32[1,8,64,128]{3,2,1,0:T(8,128)S(1)}, u32[]{:S(2)}, u32[]{:S(2)}) collective-permute-start(f32[1,8,64,128]{3,2,1,0:T(8,128)S(1)} %get-tuple-element.33), channel_id=1, source_target_pairs={{0,3},{1,2},{2,1},{3,0},{16,19},{17,18},{18,17},{19,16},{4,7},{5,6... | collective-permute-start | bytes 786440 | tf_op jit(solution)/shard_map/ppermute | solution.py:411
  655.8 23.0 %collective-permute-start.15 = (f32[1,8,64,128]{3,2,1,0:T(8,128)S(1)}, f32[1,8,64,128]{3,2,1,0:T(8,128)S(1)}, u32[]{:S(2)}, u32[]{:S(2)}) collective-permute-start(f32[1,8,64,128]{3,2,1,0:T(8,128)S(1)} %get-tuple-element.34), channel_id=1, source_target_pairs={{0,2},{1,3},{2,0},{3,1},{16,18},{17,19},{18,16},{19,17},{4,6},{5,7... | collective-permute-start | bytes 786440 | tf_op jit(solution)/shard_map/ppermute | solution.py:411
  660.7 21.4 %collective-permute-start.14 = (f32[1,8,64,128]{3,2,1,0:T(8,128)S(1)}, f32[1,8,64,128]{3,2,1,0:T(8,128)S(1)}, u32[]{:S(2)}, u32[]{:S(2)}) collective-permute-start(f32[1,8,64,128]{3,2,1,0:T(8,128)S(1)} %get-tuple-element.35), channel_id=1, source_target_pairs={{0,1},{1,0},{2,3},{3,2},{16,17},{17,16},{18,19},{19,18},{4,5},{5,4... | collective-permute-start | bytes 786440 | tf_op jit(solution)/shard_map/ppermute | solution.py:411
